TPU v7x, 256 devices: a whole 4x4x8 slice. The times are simulated.
256 devices in a mesh: row: 8 (over x, core), col: 32 (over z, y).
Axes of the slice: x: 4, y: 4, z: 8, core: 2. Of those that a mesh axis runs over, the one named last changes fastest.
Arguments:
- slab_pos: bfloat16 [64, 16384], P(None, ('row', 'col')), may hold values from -1 to 1
- slab_bias: bfloat16 [16384], P(('row', 'col')), may hold values from -1.5 to 1.5
- node_pos: bfloat16 [64, 262144], P(None, ('col', 'row')), may hold values from -1 to 1
- node_bias: bfloat16 [262144], P(('col', 'row')), may hold values from -1.5 to 1.5
- alpha: float32 [], replicated, may hold values from 6 to 7
- edge_counts: int32 [4096, 128, 128], P(('row', 'col')), may hold values from 0 to 99
- edge_blocks: int32 [4096, 2], P(('row', 'col')), may hold values from 0 to 63, as said below
Outputs:
- slab_pos_grad: float32 [64, 16384], P(None, ('row', 'col'))
- slab_bias_grad: float32 [16384], P(('row', 'col'))
- node_pos_grad: float32 [64, 262144], P(None, ('col', 'row'))
- node_bias_grad: float32 [262144], P(('col', 'row'))
Inputs may be any that keep to these rules, and one draw needn't show every extreme that they name: `edge_blocks`: within the 16 rows of one block pair (rows b * 16 to b * 16 + 15) no pair (row block, column block) repeats; the row block is below 16 and the column block below 64.
All inputs are finite; a program needn't handle non-finite values.
Results may differ from a plain program's by a relative error of at most 0.004.
Values may be sent and summed in bfloat16 or wider, within the bound.
A program may use at most 64 MiB of HBM per device.

v0:
```python
import jax
import jax.numpy as jnp
from jax import lax
from jax.sharding import PartitionSpec as P


def rates(row_pos, row_bias, col_pos, col_bias, alpha):
    rowf = row_pos.astype(jnp.float32)
    colf = col_pos.astype(jnp.float32)
    row_norm = jnp.sum(rowf * rowf, axis=0)
    col_norm = jnp.sum(colf * colf, axis=0)
    cross = lax.dot_general(
        row_pos, col_pos, (((0,), (0,)), ((), ())), preferred_element_type=jnp.float32
    )
    dist = row_norm[:, None] + col_norm[None, :] - 2.0 * cross
    eta = (
        alpha + row_bias.astype(jnp.float32)[:, None] + col_bias.astype(jnp.float32)[None, :] - dist
    )
    return jnp.exp(eta).astype(jnp.bfloat16)


def pair_sweep(row_pos, row_bias, col_pos, col_bias, alpha):
    dims, rows = row_pos.shape
    cols = col_pos.shape[1]
    width = 1024
    count = cols // width
    col_stack = col_pos.reshape(dims, count, width).transpose(1, 0, 2)
    bias_stack = col_bias.reshape(count, width)

    def sweep_step(carry, xs):
        col_blk, col_b = xs
        lam = rates(row_pos, row_bias, col_blk, col_b, alpha)
        lamf = lam.astype(jnp.float32)
        racc = carry[0] + lax.dot_general(
            col_blk, lam, (((1,), (1,)), ((), ())), preferred_element_type=jnp.float32
        )
        rtot = carry[1] + jnp.sum(lamf, axis=1)
        cacc = jnp.dot(row_pos, lam, preferred_element_type=jnp.float32)
        return ((racc, rtot), (cacc, jnp.sum(lamf, axis=0)))

    init = (jnp.zeros((dims, rows), jnp.float32), jnp.zeros((rows,), jnp.float32))
    (racc, rtot), outs = lax.scan(sweep_step, init, (col_stack, bias_stack))
    cacc = outs[0].transpose(1, 0, 2).reshape(dims, cols)
    ctot = outs[1].reshape(cols)
    return (racc, rtot, cacc, ctot)


def local(slab_pos, slab_bias, node_pos, node_bias, alpha, edge_counts, edge_blocks):
    slab_blk, slab_bblk = (
        lax.all_gather(slab_pos, "col", axis=1, tiled=True),
        lax.all_gather(slab_bias, "col", axis=0, tiled=True),
    )
    node_blk, node_bblk = (
        lax.all_gather(node_pos, "row", axis=1, tiled=True),
        lax.all_gather(node_bias, "row", axis=0, tiled=True),
    )
    dims, rows = slab_blk.shape
    cols = node_blk.shape[1]
    tile = edge_counts.shape[1]
    n_nodes = cols * lax.axis_size("col")
    n_slab = rows * lax.axis_size("row")
    rate_racc, rate_rtot, rate_cacc, rate_ctot = pair_sweep(
        slab_blk, slab_bblk, node_blk, node_bblk, alpha
    )
    counts_bf = edge_counts.astype(jnp.bfloat16)
    counts_f = edge_counts.astype(jnp.float32)
    row_ids = edge_blocks[:, 0]
    col_ids = edge_blocks[:, 1]
    slab_tiles = jnp.take(slab_blk.reshape(dims, rows // tile, tile), row_ids, axis=1)
    node_tiles = jnp.take(node_blk.reshape(dims, cols // tile, tile), col_ids, axis=1)
    row_edge = jnp.einsum("dkj,kij->dki", node_tiles, counts_bf, preferred_element_type=jnp.float32)
    col_edge = jnp.einsum("dki,kij->dkj", slab_tiles, counts_bf, preferred_element_type=jnp.float32)
    row_terms = jnp.concatenate([row_edge, jnp.sum(counts_f, axis=2)[None]], axis=0)
    col_terms = jnp.concatenate([col_edge, jnp.sum(counts_f, axis=1)[None]], axis=0)
    hi = lax.Precision.HIGHEST
    row_pick = (row_ids[:, None] == jnp.arange(rows // tile, dtype=jnp.int32)[None, :]).astype(
        jnp.float32
    )
    row_placed = jnp.einsum("eki,kt->eti", row_terms, row_pick, precision=hi).reshape(
        dims + 1, rows
    )
    row_sums = row_placed - jnp.concatenate([rate_racc, rate_rtot[None]], axis=0)
    slab_total = lax.psum_scatter(row_sums, "col", scatter_dimension=1, tiled=True)
    own_slab = slab_pos.astype(jnp.float32)
    slab_tot = slab_total[dims]
    slab_pos_grad = -2.0 * (own_slab * slab_tot[None, :] - slab_total[:dims]) / n_nodes
    slab_bias_grad = slab_tot / n_nodes
    col_pick = (col_ids[:, None] == jnp.arange(cols // tile, dtype=jnp.int32)[None, :]).astype(
        jnp.float32
    )
    col_placed = jnp.einsum("ekj,kt->etj", col_terms, col_pick, precision=hi).reshape(
        dims + 1, cols
    )
    col_sums = col_placed - jnp.concatenate([rate_cacc, rate_ctot[None]], axis=0)
    col_total = lax.psum_scatter(col_sums, "row", scatter_dimension=1, tiled=True)
    own_nodes = node_pos.astype(jnp.float32)
    node_tot = col_total[dims]
    node_pos_grad = 2.0 * (col_total[:dims] - own_nodes * node_tot[None, :]) / n_slab
    node_bias_grad = node_tot / n_slab
    return (slab_pos_grad, slab_bias_grad, node_pos_grad, node_bias_grad)


def solution(mesh):
    in_specs = (
        P(None, ("row", "col")),
        P(("row", "col")),
        P(None, ("col", "row")),
        P(("col", "row")),
        P(),
        P(("row", "col"), None, None),
        P(("row", "col"), None),
    )
    out_specs = (
        P(None, ("row", "col")),
        P(("row", "col")),
        P(None, ("col", "row")),
        P(("col", "row")),
    )
    return jax.shard_map(local, mesh=mesh, in_specs=in_specs, out_specs=out_specs, check_vma=False)
```

profile of v0, /device:TPU:1, one launch (start us, length us, event | category | flops | bytes accessed | tf_op | source)
XLA Modules:
  0.0 526.2 jit_solution(9218345092649058973)
XLA Ops:
  8.0 14.4 %all_gather.14 = bf16[8192]{0:T(1024)(128)(2,1)S(1)} all-gather(bf16[1024]{0:T(1024)(128)(2,1)} %param.12), channel_id=1, replica_groups=mesh['row'=8,'col'=32] {'row'}, dimensions={0}, use_global_device_ids=true | all-gather | bytes 18432 | tf_op jit(solution)/shard_map/all_gather | solution.py:55
  23.2 41.0 %all_gather.15 = bf16[64,2048]{0,1:T(8,128)(2,1)S(1)} all-gather(bf16[64,64]{0,1:T(8,128)(2,1)S(1)} %copy.22), channel_id=1, replica_groups=mesh['row'=8,'col'=32] {'col'}, dimensions={1}, use_global_device_ids=true | all-gather | bytes 270336 | tf_op jit(solution)/shard_map/all_gather | solution.py:50
  73.0 57.5 %all-reduce = bf16[2048]{0:T(1024)(128)(2,1)S(1)} all-reduce(bf16[2048]{0:T(1024)(128)(2,1)S(1)} %dynamic-update-slice), channel_id=1, replica_groups=mesh['row'=8,'col'=32] {'col'}, use_global_device_ids=true, to_apply=%add | all-reduce | flops 2048 | bytes 8192
  130.6 2.6 copy_bitcast_fusion
  133.1 1.8 gather_fusion
  140.5 103.2 %while.17 = (s32[]{:T(128)}, f32[64,2048]{1,0:T(8,128)S(1)}, f32[2048]{0:T(1024)S(1)}, f32[8,64,1024]{2,1,0:T(8,128)}, f32[8,1024]{1,0:T(8,128)S(1)}, /*index=5*...) while((s32[]{:T(128)}, f32[64,2048]{1,0:T(8,128)S(1)}, ...), condition=%wide.region_6.7_spmd.clone, body=%wide.region_1.6_spmd.clone.sunk | while | flops 825035776 | bytes 31951040 | solution.py:42
  142.2 5.5 %convert_reduce_fusion.5 = (f32[1024]{0:T(1024)S(1)}, f32[2048]{0:T(1024)S(1)}, bf16[2048,1024]{0,1:T(8,128)(2,1)}) fusion(bf16[64,2048]{1,0:T(8,128)(2,1)S(1)} %get-tuple-element.257, bf16[8,64,1024]{2,1,0:T(8,128)(2,1)} %get-tuple-element.253, s32[]{:T(128)S(6)} %copy.54, f32[1024]{0:T(1024)S(1)} %multiply_reduce_fusion.4, ...), kind=kOutput, calls=%fused_computation.2.clone.1 | convolution fusion | flops 287306752 | bytes 4624388 | tf_op jit(solution)/shard_map/while/body/eval_jaxpr/dot_general | solution.py:12
  147.7 3.3 convolution_add_fusion.2
  151.2 2.1 fusion.49
  155.1 5.5 %convert_reduce_fusion.5 = (f32[1024]{0:T(1024)S(1)}, f32[2048]{0:T(1024)S(1)}, bf16[2048,1024]{0,1:T(8,128)(2,1)}) fusion(bf16[64,2048]{1,0:T(8,128)(2,1)S(1)} %get-tuple-element.257, bf16[8,64,1024]{2,1,0:T(8,128)(2,1)} %get-tuple-element.253, s32[]{:T(128)S(6)} %copy.54, f32[1024]{0:T(1024)S(1)} %multiply_reduce_fusion.4, ...), kind=kOutput, calls=%fused_computation.2.clone.1 | convolution fusion | flops 287306752 | bytes 4624388 | tf_op jit(solution)/shard_map/while/body/eval_jaxpr/dot_general | solution.py:12
  160.6 3.3 convolution_add_fusion.2
  164.1 2.1 fusion.49
  168.0 5.5 %convert_reduce_fusion.5 = (f32[1024]{0:T(1024)S(1)}, f32[2048]{0:T(1024)S(1)}, bf16[2048,1024]{0,1:T(8,128)(2,1)}) fusion(bf16[64,2048]{1,0:T(8,128)(2,1)S(1)} %get-tuple-element.257, bf16[8,64,1024]{2,1,0:T(8,128)(2,1)} %get-tuple-element.253, s32[]{:T(128)S(6)} %copy.54, f32[1024]{0:T(1024)S(1)} %multiply_reduce_fusion.4, ...), kind=kOutput, calls=%fused_computation.2.clone.1 | convolution fusion | flops 287306752 | bytes 4624388 | tf_op jit(solution)/shard_map/while/body/eval_jaxpr/dot_general | solution.py:12
  173.4 3.3 convolution_add_fusion.2
  177.0 2.1 fusion.49
  180.9 5.5 %convert_reduce_fusion.5 = (f32[1024]{0:T(1024)S(1)}, f32[2048]{0:T(1024)S(1)}, bf16[2048,1024]{0,1:T(8,128)(2,1)}) fusion(bf16[64,2048]{1,0:T(8,128)(2,1)S(1)} %get-tuple-element.257, bf16[8,64,1024]{2,1,0:T(8,128)(2,1)} %get-tuple-element.253, s32[]{:T(128)S(6)} %copy.54, f32[1024]{0:T(1024)S(1)} %multiply_reduce_fusion.4, ...), kind=kOutput, calls=%fused_computation.2.clone.1 | convolution fusion | flops 287306752 | bytes 4624388 | tf_op jit(solution)/shard_map/while/body/eval_jaxpr/dot_general | solution.py:12
  186.3 3.3 convolution_add_fusion.2
  189.9 2.1 fusion.49
  193.8 5.5 %convert_reduce_fusion.5 = (f32[1024]{0:T(1024)S(1)}, f32[2048]{0:T(1024)S(1)}, bf16[2048,1024]{0,1:T(8,128)(2,1)}) fusion(bf16[64,2048]{1,0:T(8,128)(2,1)S(1)} %get-tuple-element.257, bf16[8,64,1024]{2,1,0:T(8,128)(2,1)} %get-tuple-element.253, s32[]{:T(128)S(6)} %copy.54, f32[1024]{0:T(1024)S(1)} %multiply_reduce_fusion.4, ...), kind=kOutput, calls=%fused_computation.2.clone.1 | convolution fusion | flops 287306752 | bytes 4624388 | tf_op jit(solution)/shard_map/while/body/eval_jaxpr/dot_general | solution.py:12
  199.3 3.3 convolution_add_fusion.2
  202.8 2.1 fusion.49
  206.7 5.5 %convert_reduce_fusion.5 = (f32[1024]{0:T(1024)S(1)}, f32[2048]{0:T(1024)S(1)}, bf16[2048,1024]{0,1:T(8,128)(2,1)}) fusion(bf16[64,2048]{1,0:T(8,128)(2,1)S(1)} %get-tuple-element.257, bf16[8,64,1024]{2,1,0:T(8,128)(2,1)} %get-tuple-element.253, s32[]{:T(128)S(6)} %copy.54, f32[1024]{0:T(1024)S(1)} %multiply_reduce_fusion.4, ...), kind=kOutput, calls=%fused_computation.2.clone.1 | convolution fusion | flops 287306752 | bytes 4624388 | tf_op jit(solution)/shard_map/while/body/eval_jaxpr/dot_general | solution.py:12
  212.2 3.3 convolution_add_fusion.2
  215.7 2.1 fusion.49
  219.6 5.5 %convert_reduce_fusion.5 = (f32[1024]{0:T(1024)S(1)}, f32[2048]{0:T(1024)S(1)}, bf16[2048,1024]{0,1:T(8,128)(2,1)}) fusion(bf16[64,2048]{1,0:T(8,128)(2,1)S(1)} %get-tuple-element.257, bf16[8,64,1024]{2,1,0:T(8,128)(2,1)} %get-tuple-element.253, s32[]{:T(128)S(6)} %copy.54, f32[1024]{0:T(1024)S(1)} %multiply_reduce_fusion.4, ...), kind=kOutput, calls=%fused_computation.2.clone.1 | convolution fusion | flops 287306752 | bytes 4624388 | tf_op jit(solution)/shard_map/while/body/eval_jaxpr/dot_general | solution.py:12
  225.1 3.3 convolution_add_fusion.2
  228.6 2.1 fusion.49
  232.5 5.5 %convert_reduce_fusion.5 = (f32[1024]{0:T(1024)S(1)}, f32[2048]{0:T(1024)S(1)}, bf16[2048,1024]{0,1:T(8,128)(2,1)}) fusion(bf16[64,2048]{1,0:T(8,128)(2,1)S(1)} %get-tuple-element.257, bf16[8,64,1024]{2,1,0:T(8,128)(2,1)} %get-tuple-element.253, s32[]{:T(128)S(6)} %copy.54, f32[1024]{0:T(1024)S(1)} %multiply_reduce_fusion.4, ...), kind=kOutput, calls=%fused_computation.2.clone.1 | convolution fusion | flops 287306752 | bytes 4624388 | tf_op jit(solution)/shard_map/while/body/eval_jaxpr/dot_general | solution.py:12
  238.0 3.3 convolution_add_fusion.2
  241.5 2.1 fusion.49
  249.8 226.4 %reduce-scatter.7.cloned.1.call-done = f32[64,65]{1,0:T(8,128)} async-done(((f32[2048,65]{1,0:T(8,128)}), f32[64,65]{1,0:T(8,128)}) %reduce-scatter.7.cloned.1.call-update) | async-done | bytes 16656
  479.0 37.6 %reduce-scatter.5.cloned.1.call-done = f32[65,1024]{1,0:T(8,128)} async-done(((f32[65,8192]{1,0:T(8,128)}), f32[65,1024]{1,0:T(8,128)}) %reduce-scatter.5.cloned.1.call-update) | async-done | bytes 266256 | tf_op jit(solution)/shard_map/reduce_scatter | solution.py:95
  (125 shorter events, 42.5 us)
Async XLA Ops:
  7.2 61.2 %copy-start.1 = (s32[16,128,128]{2,1,0:T(8,128)S(1)}, s32[16,128,128]{2,1,0:T(8,128)}, u32[]{:S(2)}) copy-start(s32[16,128,128]{2,1,0:T(8,128)} %param.14) | copy-start | bytes 3145732
  7.2 123.4 %all-gather.2.cloned.1.call-start = ((), (), s32[]{:S(2)}) async-start(), calls=%async_computation.2 | async-start | bytes 1179648 | tf_op jit(solution)/shard_map/all_gather | solution.py:54
  7.9 468.2 %reduce-scatter.7.cloned.1.call-start = ((), (), s32[]{:S(2)}) async-start(), calls=%async_computation.4 | async-start | bytes 1081344
  69.8 1.7 copy-start.6
  69.9 2.9 copy-start.5
  135.0 3.3 copy-start.2
  147.7 3.5 copy-start
  160.5 3.5 copy-start
  173.4 3.5 copy-start
  186.3 3.5 copy-start
  199.3 3.5 copy-start
  212.2 3.5 copy-start
  225.1 3.5 copy-start
  238.0 3.5 copy-start
  246.2 270.4 %reduce-scatter.5.cloned.1.call-start = ((), (), s32[]{:S(2)}) async-start(), calls=%async_computation.3 | async-start | bytes 2654208 | tf_op jit(solution)/shard_map/reduce_scatter | solution.py:95
  248.0 230.4 %copy-start.4 = (bf16[64,64]{1,0:T(8,128)(2,1)S(1)}, bf16[64,64]{1,0:T(8,128)(2,1)}, u32[]{:S(2)}) copy-start(bf16[64,64]{1,0:T(8,128)(2,1)} %param.9) | copy-start | bytes 24580
  248.0 269.9 %copy-start.3 = (bf16[64,1024]{1,0:T(8,128)(2,1)S(1)}, bf16[64,1024]{1,0:T(8,128)(2,1)}, u32[]{:S(2)}) copy-start(bf16[64,1024]{1,0:T(8,128)(2,1)} %param.11) | copy-start | bytes 393220
Sparse Core Ops, SparseCore 0:
  9.8 30.1 all-gather.1
  246.3 229.7 reduce-scatter.6
  478.7 37.8 reduce-scatter.4
where the time goes:
time: 529 us; the launch traced here: 526 us
  waiting for transfers between devices  265 us (50%)
  blocking collectives  113 us (21%)
  matrix products  91 us (17%)
  other arithmetic  23 us (4%)
  local copies, waits for them, and re-layouts  19.4 us (4%)
  between operations  14.7 us (3%)
    unnamed x4, waiting for transfers between devices  227 us
    unnamed x1, blocking collectives  57.5 us
    dot_general x8, matrix products, rates(): lax.dot_general(row_pos, col_pos, (((0,), (0,)), ((), ())), preferred_ele...  43.9 us
    all_gather x1, blocking collectives, local(): lax.all_gather(slab_pos, 'col', axis=1, tiled=True)  41 us
    reduce_scatter x1, waiting for transfers between devices, local(): lax.psum_scatter(col_sums, 'row', scatter_dimension=1, tiled=True)  37.6 us
    dot_general x8, matrix products, sweep_step(): lax.dot_general(col_blk, lam, (((1,), (1,)), ((), ())), preferred_element...  26.5 us
    dot_general x8, matrix products, sweep_step(): cacc = jnp.dot(row_pos, lam, preferred_element_type=jnp.float32)  16.9 us
    all_gather x1, blocking collectives, local(): lax.all_gather(node_bias, 'row', axis=0, tiled=True)  14.4 us
  transfers between devices with their start and end apart: 3, of which 2 were waited for; matrix products, arithmetic and copies ran while one was open for 3% of the time, Pallas kernels for 0%

commit v1 on v0

v1 whole, which is shorter than its diff:
```python
import functools

import jax
import jax.numpy as jnp
from jax import lax
from jax.experimental import pallas as pl
from jax.experimental.pallas import tpu as pltpu
from jax.sharding import PartitionSpec as P

MESH = pl.DeviceIdType.MESH
F32 = jnp.float32
BF16 = jnp.bfloat16
LOG2E = 1.4426950408889634
NX, NY, NZ = 4, 4, 8
XD = YD = (1, 3, 2)
ZD = (1, 7, 2, 6, 3, 5, 4)
PB, QB = 512, 1024
KROWS = 80
OROWS = 72
VMEM_LIMIT = 52 * 1024 * 1024


def split3(v):
    a = v.astype(BF16).astype(F32)
    b = (v - a).astype(BF16).astype(F32)
    c = (v - a - b).astype(BF16).astype(F32)
    return a, b, c


def extras(scalars):
    a, b, c = split3(scalars)
    i = lax.broadcasted_iota(jnp.int32, (16, scalars.shape[1]), 0)
    one = jnp.where((i == 0) | (i == 4) | (i == 5), 1.0, 0.0)
    ext = jnp.where(i == 1, a, jnp.where(i == 2, b, jnp.where(i == 3, c, one)))
    return ext.astype(BF16)


def position():
    row, col = lax.axis_index("row"), lax.axis_index("col")
    return row // 2, row % 2, col % NY, col // NY


def enter(peers):
    barrier = pltpu.get_barrier_semaphore()
    for peer in peers:
        pl.semaphore_signal(barrier, inc=1, device_id=peer, device_id_type=MESH)
    pl.semaphore_wait(barrier, len(peers))


def all_peers():
    x, core, y, z = position()
    row, col = lax.axis_index("row"), lax.axis_index("col")
    xs = {d: {"row": (x + d) % NX * 2 + core, "col": col} for d in XD}
    sibling = {"row": x * 2 + 1 - core, "col": col}
    ys = {d: {"row": row, "col": z * NY + (y + d) % NY} for d in YD}
    zs = {d: {"row": row, "col": (z + d) % NZ * NY + y} for d in ZD}
    return xs, sibling, ys, zs


def remote(src, dst, ssem, rsem, peer):
    return pltpu.make_async_remote_copy(
        src_ref=src, dst_ref=dst, send_sem=ssem, recv_sem=rsem, device_id=peer, device_id_type=MESH
    )


def columns(ref, index, width):
    return ref.at[:, pl.ds(pl.multiple_of(index * width, 128), width)]


def gather_kernel(
    alpha_ref, spos_ref, sbias_ref, npos_ref, nbias_ref, s_ref, n_ref,
    ypiece, n_send, n_recv, f_send, f_recv, y_send, y_recv, z_send, z_recv,
):
    x, core, y, z = position()
    xs, sibling, ys, zs = all_peers()
    width = npos_ref.shape[1]
    enter([xs[d] for d in XD] + [sibling] + [ys[d] for d in YD] + [zs[d] for d in ZD])

    sp = spos_ref[...].astype(F32)
    u = LOG2E * (alpha_ref[0, 0] + sbias_ref[...].astype(F32) - jnp.sum(sp * sp, axis=0, keepdims=True))
    ypiece[y] = jnp.zeros((KROWS, 128), BF16)
    ypiece[y, 0:64, 0:64] = spos_ref[...]
    ypiece[y, 64:80, 0:64] = extras(u)
    ycopies = {d: remote(ypiece.at[y], ypiece.at[y], y_send.at[d], y_recv.at[d], ys[d]) for d in YD}
    for d in YD:
        ycopies[d].start()

    nodes = npos_ref[...].astype(F32)
    v = LOG2E * (nbias_ref[...].astype(F32) - jnp.sum(nodes * nodes, axis=0, keepdims=True))
    mine = columns(n_ref, x * 2 + core, width)
    mine[0:64, :] = npos_ref[...]
    mine[64:80, :] = extras(v)
    ncopies = {d: remote(mine, mine, n_send.at[d], n_recv.at[d], xs[d]) for d in XD}
    for d in XD:
        ncopies[d].start()
    fcopies = {0: remote(mine, mine, f_send.at[0], f_recv.at[0], sibling)}
    fcopies[0].start()

    for d in YD:
        ycopies[d].wait_recv()
    lane = lax.broadcasted_iota(jnp.int32, (KROWS, 128), 1)
    zv = columns(s_ref, z, 256)
    for h in range(2):
        a, b = ypiece[2 * h].astype(F32), ypiece[2 * h + 1].astype(F32)
        zv[:, h * 128 : h * 128 + 128] = jnp.where(lane < 64, a, pltpu.roll(b, 64, 1)).astype(BF16)
    zcopies = {d: remote(zv, zv, z_send.at[d], z_recv.at[d], zs[d]) for d in ZD}
    for d in ZD:
        zcopies[d].start()

    for d in XD:
        ncopies[d].wait_recv()
        piece = columns(n_ref, (x + NX - d) % NX * 2 + core, width)
        fcopies[d] = remote(piece, piece, f_send.at[d], f_recv.at[d], sibling)
        fcopies[d].start()
    for group in (fcopies, zcopies):
        for d in group:
            group[d].wait_recv()
    for group in (ycopies, ncopies, fcopies, zcopies):
        for d in group:
            group[d].wait_send()


def local_kernel(blocks_ref, counts_ref, s_ref, n_ref, r_ref, c_ref, a_ref, nt_ref, racc):
    rows, cols = s_ref.shape[1], n_ref.shape[1]
    for i in range(rows // 256):
        sl = pl.ds(i * 256, 256)
        s = s_ref[:, sl].astype(F32)
        h1, h2, h3 = split3(s[0:64] * (2.0 * LOG2E))
        k = lax.broadcasted_iota(jnp.int32, (16, 256), 0)
        one = jnp.where((k >= 1) & (k <= 3), 1.0, 0.0)
        e = jnp.where(k == 0, s[65:66], jnp.where(k == 4, s[66:67], jnp.where(k == 5, s[67:68], one)))
        t = jnp.concatenate([h1, h2, h3, e, jnp.zeros((48, 256), F32)], axis=0)
        a_ref[sl, :] = t.T.astype(BF16)
    racc[...] = jnp.zeros_like(racc)

    def chunk(j, _):
        q = pl.ds(pl.multiple_of(j * QB, 128), QB)
        n = n_ref[:, q]
        b = jnp.concatenate([n[0:64], n[0:64], n, jnp.zeros((48, QB), BF16)], axis=0)
        nt = jnp.concatenate([n.astype(F32), jnp.zeros((48, QB), F32)], axis=0).T.astype(BF16)
        nt_ref[q, :] = nt
        cacc = jnp.zeros((KROWS, QB), F32)
        for i in range(rows // PB):
            sl = pl.ds(i * PB, PB)
            t = jnp.dot(a_ref[sl, :], b, preferred_element_type=F32)
            lam = jnp.exp2(t).astype(BF16)
            racc[sl, :] -= jnp.dot(lam, nt, preferred_element_type=F32)
            cacc += jnp.dot(s_ref[:, sl], lam, preferred_element_type=F32)
        c_ref[:, q] = -cacc[0:OROWS]
        return 0

    lax.fori_loop(0, cols // QB, chunk, 0)

    def edge(k, _):
        p = pl.ds(pl.multiple_of(blocks_ref[k, 0] * 128, 128), 128)
        q = pl.ds(pl.multiple_of(blocks_ref[k, 1] * 128, 128), 128)
        y = counts_ref[k].astype(F32).astype(BF16)
        racc[p, :] += jnp.dot(y, nt_ref[q, :], preferred_element_type=F32)
        c_ref[:, q] += jnp.dot(s_ref[:, p], y, preferred_element_type=F32)[0:OROWS]
        return 0

    lax.fori_loop(0, counts_ref.shape[0], edge, 0)
    for i in range(rows // 256):
        sl = pl.ds(i * 256, 256)
        r_ref[:, sl] = racc[sl, :].T[0:OROWS]


def scatter_kernel(
    spos_ref, npos_ref, r_ref, c_ref, sg_ref, sb_ref, ng_ref, nb_ref,
    sib, xbuf, xin, zin, yblk, yin, f_send, f_recv, x_send, x_recv, z_send, z_recv, y_send, y_recv,
    *, n_nodes, n_slab,
):
    x, core, y, z = position()
    xs, sibling, ys, zs = all_peers()
    width = npos_ref.shape[1]
    enter([xs[d] for d in XD] + [sibling] + [ys[d] for d in YD] + [zs[d] for d in ZD])

    zcopies = {}
    for d in ZD:
        zcopies[d] = remote(columns(r_ref, (z + d) % NZ, 256), zin.at[d], z_send.at[d], z_recv.at[d], zs[d])
        zcopies[d].start()
    scopies, xcopies = {}, {}
    for d in XD + (0,):
        src = columns(c_ref, (x + d) % NX * 2 + 1 - core, width)
        scopies[d] = remote(src, sib.at[d], f_send.at[d], f_recv.at[d], sibling)
        scopies[d].start()
    for d in XD:
        scopies[d].wait_recv()
        xbuf[d] = columns(c_ref, (x + d) % NX * 2 + core, width)[...] + sib[d]
        xcopies[d] = remote(xbuf.at[d], xin.at[d], x_send.at[d], x_recv.at[d], xs[d])
        xcopies[d].start()

    for d in ZD:
        zcopies[d].wait_recv()
    total = columns(r_ref, z, 256)[...]
    for d in ZD:
        total += zin[d]
    yblk[0] = total[:, 0:128]
    yblk[1] = total[:, 128:256]
    ycopies = {}
    for d in YD:
        ycopies[d] = remote(yblk.at[(y + d) % NY // 2], yin.at[d], y_send.at[d], y_recv.at[d], ys[d])
        ycopies[d].start()
    for d in YD:
        ycopies[d].wait_recv()
    mine = yblk[y // 2]
    for d in YD:
        mine += yin[d]
    odd = jnp.broadcast_to(y % 2, mine.shape) == 1
    mine = jnp.where(odd, pltpu.roll(mine, 64, 1), mine)[:, 0:64]
    tot = mine[64:65]
    sg_ref[...] = (spos_ref[...].astype(F32) * tot - mine[0:64]) * (-2.0 / n_nodes)
    sb_ref[...] = tot * (1.0 / n_nodes)

    scopies[0].wait_recv()
    for d in XD:
        xcopies[d].wait_recv()
    for h in range(width // 256):
        sl = pl.ds(h * 256, 256)
        acc = columns(c_ref, x * 2 + core, width)[:, sl] + sib[0, :, sl]
        for d in XD:
            acc += xin[d, :, sl]
        tot = acc[64:65]
        ng_ref[:, sl] = (acc[0:64] - npos_ref[:, sl].astype(F32) * tot) * (2.0 / n_slab)
        nb_ref[:, sl] = tot * (1.0 / n_slab)
    for group in (zcopies, scopies, xcopies, ycopies):
        for d in group:
            group[d].wait_send()


def params(**kw):
    return pltpu.CompilerParams(vmem_limit_bytes=VMEM_LIMIT, **kw)


def local(slab_pos, slab_bias, node_pos, node_bias, alpha, edge_counts, edge_blocks):
    vmem = pl.BlockSpec(memory_space=pltpu.VMEM)
    smem = pl.BlockSpec(memory_space=pltpu.SMEM)
    dma = pltpu.SemaphoreType.DMA
    own_rows, own_cols = slab_pos.shape[1], node_pos.shape[1]
    rows = own_rows * lax.axis_size("col")
    cols = own_cols * lax.axis_size("row")
    n_slab = rows * lax.axis_size("row")
    n_nodes = cols * lax.axis_size("col")
    slab, nodes = pl.pallas_call(
        gather_kernel,
        out_shape=(jax.ShapeDtypeStruct((KROWS, rows), BF16), jax.ShapeDtypeStruct((KROWS, cols), BF16)),
        in_specs=[smem, vmem, vmem, vmem, vmem],
        out_specs=(vmem, vmem),
        scratch_shapes=[pltpu.VMEM((NY, KROWS, 128), BF16)]
        + [dma((NX,))] * 4 + [dma((NY,))] * 2 + [dma((NZ,))] * 2,
        compiler_params=params(collective_id=0, has_side_effects=True),
        name="gather",
    )(alpha.reshape(1, 1), slab_pos, slab_bias.reshape(1, own_rows), node_pos, node_bias.reshape(1, own_cols))
    row_sums, col_sums = pl.pallas_call(
        local_kernel,
        out_shape=(jax.ShapeDtypeStruct((OROWS, rows), F32), jax.ShapeDtypeStruct((OROWS, cols), F32)),
        in_specs=[smem, vmem, vmem, vmem],
        out_specs=(vmem, vmem),
        scratch_shapes=[
            pltpu.VMEM((rows, 256), BF16), pltpu.VMEM((cols, 128), BF16), pltpu.VMEM((rows, 128), F32),
        ],
        compiler_params=params(),
        name="sweep",
    )(edge_blocks, edge_counts, slab, nodes)
    piece = pltpu.VMEM((NX, OROWS, own_cols), F32)
    sg, sb, ng, nb = pl.pallas_call(
        functools.partial(scatter_kernel, n_nodes=n_nodes, n_slab=n_slab),
        out_shape=(
            jax.ShapeDtypeStruct((64, own_rows), F32), jax.ShapeDtypeStruct((1, own_rows), F32),
            jax.ShapeDtypeStruct((64, own_cols), F32), jax.ShapeDtypeStruct((1, own_cols), F32),
        ),
        in_specs=[vmem] * 4,
        out_specs=(vmem,) * 4,
        scratch_shapes=[
            piece, piece, piece, pltpu.VMEM((NZ, OROWS, 256), F32),
            pltpu.VMEM((2, OROWS, 128), F32), pltpu.VMEM((NY, OROWS, 128), F32),
        ] + [dma((NX,))] * 4 + [dma((NZ,))] * 2 + [dma((NY,))] * 2,
        compiler_params=params(collective_id=1, has_side_effects=True),
        name="scatter",
    )(slab_pos, node_pos, row_sums, col_sums)
    return sg, sb.reshape(own_rows), ng, nb.reshape(own_cols)


def solution(mesh):
    in_specs = (
        P(None, ("row", "col")),
        P(("row", "col")),
        P(None, ("col", "row")),
        P(("col", "row")),
        P(),
        P(("row", "col"), None, None),
        P(("row", "col"), None),
    )
    out_specs = (
        P(None, ("row", "col")),
        P(("row", "col")),
        P(None, ("col", "row")),
        P(("col", "row")),
    )
    return jax.shard_map(local, mesh=mesh, in_specs=in_specs, out_specs=out_specs, check_vma=False)
```

time: 529 us -> 85.6 us (0.16)
  waiting for transfers between devices: 265 us -> 0 us
  blocking collectives: 113 us -> 0 us
  matrix products: 91 us -> 0 us
  Pallas kernels: 0 us -> 75.6 us
  other arithmetic: 23 us -> 0 us
  between operations: 14.7 us -> 1.31 us
  local copies, waits for them, and re-layouts: 19.4 us -> 8.43 us
    unnamed x4 -> x0, waiting for transfers between devices: 227 us -> none
    dot_general x28 -> x0, matrix products: 91 us -> none  [the longest x8 43.9 us: rates(): lax.dot_general(row_pos, col_pos, (((0,), (0,)), ((), ())), preferred_ele...]
    pallas_call x0 -> x3, Pallas kernels: none -> 75.6 us  [the longest x1 30 us: local(): pl.pallas_call(local_kernel, out_shape=(jax.ShapeDtypeStruct((OROWS, rows...]
    unnamed x1 -> x0, blocking collectives: 57.5 us -> none
    all_gather x2 -> x0, blocking collectives: 55.4 us -> none  [the longest x1 41 us: local(): lax.all_gather(slab_pos, 'col', axis=1, tiled=True)]
    reduce_scatter x1 -> x0, waiting for transfers between devices: 37.6 us -> none  [local(): lax.psum_scatter(col_sums, 'row', scatter_dimension=1, tiled=True)]
    reduce_sum x17 -> x0, other arithmetic: 9.71 us -> none  [the longest x8 7.57 us: rates(): col_norm = jnp.sum(colf * colf, axis=0)]
    add x24 -> x0, other arithmetic: 5.35 us -> none  [the longest x16 5.3 us: rates(): alpha + row_bias.astype(jnp.float32)[:, None]]
  transfers between devices with their start and end apart: 3 -> 0, of which waited for: 2 -> 0; matrix products, arithmetic and copies ran while one was open for 3% -> 0% of each run, Pallas kernels for 0% -> 0%
where the time goes in v1:
time: 85.6 us; the launch traced here: 85.3 us
  Pallas kernels  75.6 us (88%)
  local copies, waits for them, and re-layouts  8.43 us (10%)
  between operations  1.31 us (2%)
    pallas_call x1, Pallas kernels, local(): pl.pallas_call(local_kernel, out_shape=(jax.ShapeDtypeStruct((OROWS, rows...  30 us
    pallas_call x1, Pallas kernels, local(): pl.pallas_call(functools.partial(scatter_kernel, n_nodes=n_nodes, n_slab=...  25.1 us
    pallas_call x1, Pallas kernels, local(): pl.pallas_call(gather_kernel, out_shape=(jax.ShapeDtypeStruct((KROWS, row...  20.5 us
    unnamed x17, local copies, waits for them, and re-layouts  7.74 us

profile of v1, /device:TPU:1, one launch (start us, length us, event | category | flops | bytes accessed | tf_op | source)
XLA Modules:
  0.0 85.3 jit_solution(3608035756666464391)
XLA Ops:
  1.3 0.7 reshape.25.nbias_ref
  2.0 0.8 copy.11.blocks_ref
  2.7 0.0 copy-start.2
  2.7 0.9 %copy-done.2 = bf16[64,1024]{1,0:T(8,128)(2,1)S(1)} copy-done((bf16[64,1024]{1,0:T(8,128)(2,1)S(1)}, bf16[64,1024]{1,0:T(8,128)(2,1)}, u32[]{:S(2)}) %copy-start.2) | copy-done | bytes 131096
  3.6 0.0 copy-start.4
  3.6 0.7 copy-done.4
  4.3 0.0 copy-start.5
  4.3 0.7 copy-done.5
  5.0 0.0 copy-start.3
  5.0 20.5 %gather.1 = (bf16[80,2048]{1,0:T(8,128)(2,1)S(1)}, bf16[80,8192]{1,0:T(8,128)(2,1)S(1)}) custom-call(f32[1,1]{1,0:T(1,128)} %bitcast.4.alpha_ref, bf16[64,64]{1,0:T(8,128)(2,1)S(1)} %copy-done.4, bf16[1,64]{1,0:T(2,128)(2,1)S(1)} %bitcast.6, bf16[64,1024]{1,0:T(8,128)(2,1)S(1)} %copy-done.2, bf16[1,1024]{1,0:T(2,128)(2,1)S(1)} %reshape.25.nbias_ref), custom_call_target="tpu_custom_call" | custom-call | tf_op jit(solution)/shard_map/gather/pallas_call | solution.py:244
  25.5 0.0 copy-start
  25.6 1.1 %copy-done = bf16[80,8192]{1,0:T(8,128)(2,1)} copy-done((bf16[80,8192]{1,0:T(8,128)(2,1)}, bf16[80,8192]{1,0:T(8,128)(2,1)S(1)}, u32[]{:S(2)}) %copy-start) | copy-done | bytes 1310744
  26.6 0.0 copy-start.1
  26.6 1.2 %copy-done.1 = s32[16,128,128]{2,1,0:T(8,128)S(1)} copy-done((s32[16,128,128]{2,1,0:T(8,128)S(1)}, s32[16,128,128]{2,1,0:T(8,128)}, u32[]{:S(2)}) %copy-start.1) | copy-done | bytes 1048600
  27.8 30.0 %sweep.1 = (f32[72,2048]{1,0:T(8,128)S(1)}, f32[72,8192]{1,0:T(8,128)}) custom-call(s32[16,2]{1,0:T(8,128)S(1)} %copy.11.blocks_ref, s32[16,128,128]{2,1,0:T(8,128)S(1)} %copy-done.1, bf16[80,2048]{1,0:T(8,128)(2,1)S(1)} %get-tuple-element.12.s_ref, bf16[80,8192]{1,0:T(8,128)(2,1)} %copy-done), custom_call_target="tpu_custom_call" | custom-call | tf_op jit(solution)/shard_map/sweep/pallas_call | solution.py:254
  57.8 0.0 copy-done.3
  57.8 25.1 %scatter.1 = (f32[64,64]{1,0:T(8,128)S(1)}, f32[1,64]{1,0:T(1,128)S(1)}, f32[64,1024]{1,0:T(8,128)S(1)}, f32[1,1024]{1,0:T(1,128)S(1)}) custom-call(bf16[64,64]{1,0:T(8,128)(2,1)S(1)} %copy-done.4, bf16[64,1024]{1,0:T(8,128)(2,1)S(1)} %copy-done.3, f32[72,2048]{1,0:T(8,128)S(1)} %get-tuple-element.14.r_ref, f32[72,8192]{1,0:T(8,128)} %get-tuple-element.15.c_ref), custom_call_target="tpu_custom_call" | custom-call | tf_op jit(solution)/shard_map/scatter/pallas_call | solution.py:266
  82.9 0.6 copy.17
  83.5 0.5 copy.18
  84.0 0.7 copy.19
  84.7 0.6 copy.20
Async XLA Ops:
  2.7 0.9 %copy-start.2 = (bf16[64,1024]{1,0:T(8,128)(2,1)S(1)}, bf16[64,1024]{1,0:T(8,128)(2,1)}, u32[]{:S(2)}) copy-start(bf16[64,1024]{1,0:T(8,128)(2,1)} %npos_ref.3) | copy-start | bytes 393220
  3.6 0.7 copy-start.4
  4.3 0.7 copy-start.5
  5.0 52.8 %copy-start.3 = (bf16[64,1024]{1,0:T(8,128)(2,1)S(1)}, bf16[64,1024]{1,0:T(8,128)(2,1)}, u32[]{:S(2)}) copy-start(bf16[64,1024]{1,0:T(8,128)(2,1)} %npos_ref.3) | copy-start | bytes 393220
  25.5 1.1 %copy-start = (bf16[80,8192]{1,0:T(8,128)(2,1)}, bf16[80,8192]{1,0:T(8,128)(2,1)S(1)}, u32[]{:S(2)}) copy-start(bf16[80,8192]{1,0:T(8,128)(2,1)S(1)} %get-tuple-element.13.n_ref) | copy-start | bytes 3932164
  26.6 1.2 %copy-start.1 = (s32[16,128,128]{2,1,0:T(8,128)S(1)}, s32[16,128,128]{2,1,0:T(8,128)}, u32[]{:S(2)}) copy-start(s32[16,128,128]{2,1,0:T(8,128)} %counts_ref.1) | copy-start | bytes 3145732

commit v2 on v1

v2 whole, which is shorter than its diff:
```python
import functools

import jax
import jax.numpy as jnp
from jax import lax
from jax.experimental import pallas as pl
from jax.experimental.pallas import tpu as pltpu
from jax.sharding import PartitionSpec as P

MESH = pl.DeviceIdType.MESH
F32 = jnp.float32
BF16 = jnp.bfloat16
LOG2E = 1.4426950408889634
NX, NY, NZ = 4, 4, 8
XD = YD = (1, 3, 2)
ZD = (1, 7, 2, 6, 3, 5, 4)
ORDER = (4, 3, 5, 2, 6, 7, 1, 0)
SLOT = {d: s for s, d in enumerate(ORDER)}
PB, QB = 512, 1024
TB = 128
KROWS = 80
OROWS = 72
VMEM_LIMIT = 52 * 1024 * 1024


def split3(v):
    a = v.astype(BF16).astype(F32)
    b = (v - a).astype(BF16).astype(F32)
    c = (v - a - b).astype(BF16).astype(F32)
    return a, b, c


def extras(scalars):
    a, b, c = split3(scalars)
    i = lax.broadcasted_iota(jnp.int32, (16, scalars.shape[1]), 0)
    one = jnp.where((i == 0) | (i == 4) | (i == 5), 1.0, 0.0)
    ext = jnp.where(i == 1, a, jnp.where(i == 2, b, jnp.where(i == 3, c, one)))
    return ext.astype(BF16)


def position():
    row, col = lax.axis_index("row"), lax.axis_index("col")
    return row // 2, row % 2, col % NY, col // NY


def enter(peers):
    barrier = pltpu.get_barrier_semaphore()
    for peer in peers:
        pl.semaphore_signal(barrier, inc=1, device_id=peer, device_id_type=MESH)
    pl.semaphore_wait(barrier, len(peers))


def all_peers():
    x, core, y, z = position()
    row, col = lax.axis_index("row"), lax.axis_index("col")
    xs = {d: {"row": (x + d) % NX * 2 + core, "col": col} for d in XD}
    sibling = {"row": x * 2 + 1 - core, "col": col}
    ys = {d: {"row": row, "col": z * NY + (y + d) % NY} for d in YD}
    zs = {d: {"row": row, "col": (z + d) % NZ * NY + y} for d in ZD}
    return xs, sibling, ys, zs


def remote(src, dst, ssem, rsem, peer):
    return pltpu.make_async_remote_copy(
        src_ref=src, dst_ref=dst, send_sem=ssem, recv_sem=rsem, device_id=peer, device_id_type=MESH
    )


def columns(ref, index, width):
    return ref.at[:, pl.ds(pl.multiple_of(index * width, 128), width)]


def params(**kw):
    return pltpu.CompilerParams(vmem_limit_bytes=VMEM_LIMIT, **kw)


def body(
    blocks_ref, alpha_ref, sbias_ref, nbias_ref, spos_hbm, npos_hbm, counts_hbm,
    sg_ref, sb_ref, ng_ref, nb_ref,
    spos_ref, npos_ref, counts_ref, in_sem,
    s_ref, n_ref, nt_ref, st_ref, a_ref, racc, cacc, erow, ecol,
    ypiece, sib, xbuf, xin, zout, zin, yblk, yin,
    n_send, n_recv, f_send, f_recv, y_send, y_recv, z_send, z_recv,
    cf_send, cf_recv, cx_send, cx_recv, rz_send, rz_recv, ry_send, ry_recv,
    *, n_nodes, n_slab,
):
    x, core, y, z = position()
    xs, sibling, ys, zs = all_peers()
    width = npos_ref.shape[1]
    tiles = counts_ref.shape[0]
    copies = []

    def send(src, dst, ssem, rsem, peer):
        c = remote(src, dst, ssem, rsem, peer)
        c.start()
        copies.append(c)
        return c

    loads = [
        pltpu.make_async_copy(a, b, in_sem.at[i])
        for i, (a, b) in enumerate(((spos_hbm, spos_ref), (npos_hbm, npos_ref), (counts_hbm, counts_ref)))
    ]
    for c in loads:
        c.start()
    enter([xs[d] for d in XD] + [sibling] + [ys[d] for d in YD] + [zs[d] for d in ZD])

    loads[0].wait()
    sp = spos_ref[...].astype(F32)
    u = LOG2E * (alpha_ref[0, 0] + sbias_ref[...].astype(F32) - jnp.sum(sp * sp, axis=0, keepdims=True))
    ypiece[y] = jnp.zeros((KROWS, 128), BF16)
    ypiece[y, 0:64, 0:64] = spos_ref[...]
    ypiece[y, 64:80, 0:64] = extras(u)
    yget = {d: send(ypiece.at[y], ypiece.at[y], y_send.at[d], y_recv.at[d], ys[d]) for d in YD}

    loads[1].wait()
    nodes = npos_ref[...].astype(F32)
    nb = nbias_ref[...].astype(F32)
    nb = jnp.concatenate([nb[i : i + 1] for i in range(width // 128)], axis=1)
    v = LOG2E * (nb - jnp.sum(nodes * nodes, axis=0, keepdims=True))
    mine = columns(n_ref, x * 2 + core, width)
    mine[0:64, :] = npos_ref[...]
    mine[64:80, :] = extras(v)
    nget = {d: send(mine, mine, n_send.at[d], n_recv.at[d], xs[d]) for d in XD}
    f0 = send(mine, mine, f_send.at[0], f_recv.at[0], sibling)

    racc[...] = jnp.zeros_like(racc)
    cacc[...] = jnp.zeros_like(cacc)

    for d in YD:
        yget[d].wait_recv()
    lane = lax.broadcasted_iota(jnp.int32, (KROWS, 128), 1)
    own = s_ref.at[:, pl.ds(SLOT[0] * 256, 256)]
    for h in range(2):
        a, b = ypiece[2 * h].astype(F32), ypiece[2 * h + 1].astype(F32)
        own[:, h * 128 : h * 128 + 128] = jnp.where(lane < 64, a, pltpu.roll(b, 64, 1)).astype(BF16)
    zget = {}
    for d in ORDER[:-1]:
        dst = s_ref.at[:, pl.ds(SLOT[d] * 256, 256)]
        zget[d] = send(own, dst, z_send.at[d], z_recv.at[d], zs[d])

    def prep_rows(slot):
        sl = pl.ds(slot * 256, 256)
        s = s_ref[:, sl].astype(F32)
        h1, h2, h3 = split3(s[0:64] * (2.0 * LOG2E))
        k = lax.broadcasted_iota(jnp.int32, (16, 256), 0)
        one = jnp.where((k >= 1) & (k <= 3), 1.0, 0.0)
        e = jnp.where(k == 0, s[65:66], jnp.where(k == 4, s[66:67], jnp.where(k == 5, s[67:68], one)))
        t = jnp.concatenate([h1, h2, h3, e, jnp.zeros((48, 256), F32)], axis=0)
        a_ref[sl, :] = t.T.astype(BF16)

    def chunk(j):
        return pl.ds(pl.multiple_of(j * QB, QB), QB)

    def prep_cols(j):
        n = n_ref[:, chunk(j)]
        t = jnp.concatenate([n.astype(F32), jnp.zeros((48, QB), F32)], axis=0).T.astype(BF16)
        nt_ref[pl.ds(j * (QB // TB), QB // TB)] = t.reshape(QB // TB, TB, 128)

    def unit(pair, j):
        q = chunk(j)
        sl = pl.ds(pl.multiple_of(pair * PB, PB), PB)
        n = n_ref[:, q]
        b = jnp.concatenate([n[0:64], n[0:64], n, jnp.zeros((48, QB), BF16)], axis=0)
        t = jnp.dot(a_ref[sl, :], b, preferred_element_type=F32)
        lam = jnp.exp2(t).astype(BF16)
        racc[sl, :] -= jnp.dot(
            lam, nt_ref[pl.ds(j * (QB // TB), QB // TB)].reshape(QB, 128), preferred_element_type=F32
        )
        cacc[:, q] -= jnp.dot(s_ref[:, sl], lam, preferred_element_type=F32)[0:OROWS]

    def spans(n, f):
        def step(i, _):
            f(i)
            return 0

        lax.fori_loop(0, n, step, 0)

    def chip(d):
        return (x + d) % NX

    for d in ORDER[0:2]:
        zget[d].wait_recv()
        prep_rows(SLOT[d])

    def first_own(i):
        j = x * 2 + (core + i) % 2

        @pl.when(i == 1)
        def _():
            f0.wait_recv()

        prep_cols(j)
        unit(0, j)

    spans(2, first_own)

    def first_others(i):
        d = 1 + i // 2
        src = chip(NX - d)
        h = i % 2

        @pl.when(h == 0)
        def _():
            piece = columns(n_ref, src * 2 + core, width)
            remote(piece, piece, n_send.at[d], n_recv.at[d], sibling).wait_recv()
            remote(piece, piece, f_send.at[d], f_recv.at[d], sibling).start()

        @pl.when(h == 1)
        def _():
            piece = columns(n_ref, src * 2 + 1 - core, width)
            remote(piece, piece, f_send.at[d], f_recv.at[d], sibling).wait_recv()

        j = src * 2 + (core + h) % 2
        prep_cols(j)
        unit(0, j)

    spans(6, first_others)
    for d in XD:
        piece = columns(n_ref, chip(NX - d) * 2 + core, width)
        copies.append(remote(piece, piece, f_send.at[d], f_recv.at[d], sibling))

    for d in ORDER[2:-1]:
        zget[d].wait_recv()
    for d in ORDER[2:]:
        prep_rows(SLOT[d])

    loads[2].wait()

    for d in ORDER:
        for h in range(2):
            st_ref[(z + NZ - d) % NZ * 2 + h] = s_ref[:, pl.ds(SLOT[d] * 256 + h * TB, TB)]

    def edge(k):
        yk = counts_ref[k].astype(F32).astype(BF16)
        erow[k] = jnp.dot(yk, nt_ref[blocks_ref[1, k]], preferred_element_type=F32)
        ecol[k] = jnp.dot(st_ref[blocks_ref[0, k]], yk, preferred_element_type=F32)[0:OROWS]

    def same(a, b):
        return (1 - jnp.minimum((a - b) * (a - b), 1)).astype(F32)

    spans(tiles, edge)

    def place_cols(t):
        q = pl.ds(pl.multiple_of(t * TB, TB), TB)
        acc = cacc[:, q]
        for k in range(tiles):
            acc += same(blocks_ref[1, k], t) * ecol[k]
        cacc[:, q] = acc

    spans(cacc.shape[1] // TB, place_cols)

    def rows_done(slot):
        d = ORDER[slot]
        parts = []
        for h in range(2):
            acc = racc[pl.ds(slot * 256 + h * TB, TB), :]
            for k in range(tiles):
                acc += same(blocks_ref[0, k], (z + NZ - d) % NZ * 2 + h) * erow[k]
            parts.append(acc)
        return jnp.concatenate(parts, axis=0).T[0:OROWS]

    rget = {}

    def rows_out(slot):
        e = (NZ - ORDER[slot]) % NZ
        zout[e] = rows_done(slot)
        rget[e] = send(zout.at[e], zin.at[e], rz_send.at[e], rz_recv.at[e], zs[e])

    cget, xget = {}, {}

    def cols_other(d):
        src = columns(cacc, chip(d) * 2 + 1 - core, width)
        cget[d] = send(src, sib.at[d], cf_send.at[d], cf_recv.at[d], sibling)

    def cols_out(d):
        cget[d].wait_recv()
        xbuf[d] = columns(cacc, chip(d) * 2 + core, width)[...] + sib[d]
        xget[d] = send(xbuf.at[d], xin.at[d], cx_send.at[d], cx_recv.at[d], xs[d])

    def cols_of(d, first, n):
        spans(n, lambda i: unit(first + i, chip(d) * 2 + 1 - core))
        cols_other(d)
        spans(n, lambda i: unit(first + i, chip(d) * 2 + core))
        cols_out(d)

    rows_out(0)
    rows_out(1)
    cols_of(2, 1, 3)
    spans(6, lambda i: unit(1, chip(3 + i // 2) * 2 + i % 2))
    rows_out(2)
    rows_out(3)
    cols_of(1, 2, 2)
    cols_of(3, 2, 2)
    spans(2, lambda i: unit(2, x * 2 + (core + 1 + i) % 2))
    rows_out(4)
    rows_out(5)
    unit(3, x * 2 + 1 - core)
    cols_other(0)
    unit(3, x * 2 + core)
    rows_out(6)

    total = rows_done(7)
    for e in (4, 5, 3, 6, 2, 1, 7):
        rget[e].wait_recv()
        total += zin[e]
    yblk[0] = total[:, 0:128]
    yblk[1] = total[:, 128:256]
    yback = {d: send(yblk.at[(y + d) % NY // 2], yin.at[d], ry_send.at[d], ry_recv.at[d], ys[d]) for d in YD}

    cget[0].wait_recv()
    for d in XD:
        xget[d].wait_recv()
    for h in range(width // 256):
        sl = pl.ds(h * 256, 256)
        acc = columns(cacc, x * 2 + core, width)[:, sl] + sib[0, :, sl]
        for d in XD:
            acc += xin[d, :, sl]
        tot = acc[64:65]
        ng_ref[:, sl] = (acc[0:64] - npos_ref[:, sl].astype(F32) * tot) * (2.0 / n_slab)
        nb_ref[:, sl] = tot * (1.0 / n_slab)

    for d in YD:
        yback[d].wait_recv()
    own_sums = yblk[y // 2]
    for d in YD:
        own_sums += yin[d]
    odd = jnp.broadcast_to(y % 2, own_sums.shape) == 1
    own_sums = jnp.where(odd, pltpu.roll(own_sums, 64, 1), own_sums)[:, 0:64]
    tot = own_sums[64:65]
    sg_ref[...] = (spos_ref[...].astype(F32) * tot - own_sums[0:64]) * (-2.0 / n_nodes)
    sb_ref[...] = tot * (1.0 / n_nodes)
    for c in copies:
        c.wait_send()


def local(slab_pos, slab_bias, node_pos, node_bias, alpha, edge_counts, edge_blocks):
    vmem = pl.BlockSpec(memory_space=pltpu.VMEM)
    smem = pl.BlockSpec(memory_space=pltpu.SMEM)
    hbm = pl.BlockSpec(memory_space=pl.ANY)
    dma = pltpu.SemaphoreType.DMA
    own_rows, own_cols = slab_pos.shape[1], node_pos.shape[1]
    rows = own_rows * lax.axis_size("col")
    cols = own_cols * lax.axis_size("row")
    n_slab = rows * lax.axis_size("row")
    n_nodes = cols * lax.axis_size("col")
    tiles = edge_counts.shape[0]
    piece = pltpu.VMEM((NX, OROWS, own_cols), F32)
    group = pltpu.VMEM((NZ, OROWS, 256), F32)
    sg, sb, ng, nb = pl.pallas_call(
        functools.partial(body, n_nodes=n_nodes, n_slab=n_slab),
        out_shape=(
            jax.ShapeDtypeStruct((64, own_rows), F32), jax.ShapeDtypeStruct((1, own_rows), F32),
            jax.ShapeDtypeStruct((64, own_cols), F32), jax.ShapeDtypeStruct((1, own_cols), F32),
        ),
        in_specs=[smem, smem, vmem, vmem, hbm, hbm, hbm],
        out_specs=(vmem,) * 4,
        scratch_shapes=[
            pltpu.VMEM(slab_pos.shape, BF16), pltpu.VMEM(node_pos.shape, BF16),
            pltpu.VMEM(edge_counts.shape, jnp.int32), dma((3,)),
            pltpu.VMEM((KROWS, rows), BF16), pltpu.VMEM((KROWS, cols), BF16), pltpu.VMEM((cols // TB, TB, 128), BF16),
            pltpu.VMEM((rows // TB, KROWS, TB), BF16),
            pltpu.VMEM((rows, 256), BF16), pltpu.VMEM((rows, 128), F32), pltpu.VMEM((OROWS, cols), F32),
            pltpu.VMEM((tiles, TB, 128), F32), pltpu.VMEM((tiles, OROWS, TB), F32),
            pltpu.VMEM((NY, KROWS, 128), BF16), piece, piece, piece, group, group,
            pltpu.VMEM((2, OROWS, 128), F32), pltpu.VMEM((NY, OROWS, 128), F32),
        ] + [dma((NX,))] * 4 + [dma((NY,))] * 2 + [dma((NZ,))] * 2
        + [dma((NX,))] * 4 + [dma((NZ,))] * 2 + [dma((NY,))] * 2,
        compiler_params=params(collective_id=0, has_side_effects=True),
        name="gradient",
    )(
        edge_blocks.T, alpha.reshape(1, 1), slab_bias.reshape(1, own_rows), node_bias.reshape(own_cols // 128, 128),
        slab_pos, node_pos, edge_counts,
    )
    return sg, sb.reshape(own_rows), ng, nb.reshape(own_cols)


def solution(mesh):
    in_specs = (
        P(None, ("row", "col")),
        P(("row", "col")),
        P(None, ("col", "row")),
        P(("col", "row")),
        P(),
        P(("row", "col"), None, None),
        P(("row", "col"), None),
    )
    out_specs = (
        P(None, ("row", "col")),
        P(("row", "col")),
        P(None, ("col", "row")),
        P(("col", "row")),
    )
    return jax.shard_map(local, mesh=mesh, in_specs=in_specs, out_specs=out_specs, check_vma=False)
```

time: 85.6 us -> 74.9 us (0.88)
  Pallas kernels: 75.6 us -> 67.4 us
  local copies, waits for them, and re-layouts: 8.43 us -> 5.94 us
    pallas_call x3 -> x1, Pallas kernels: 75.6 us -> 67.4 us  [local(): pl.pallas_call(functools.partial(body, n_nodes=n_nodes, n_slab=n_slab), o...]
    unnamed x17 -> x16, local copies, waits for them, and re-layouts: 7.74 us -> 5.94 us
where the time goes in v2:
time: 74.9 us; the launch traced here: 74.6 us
  Pallas kernels  67.4 us (90%)
  local copies, waits for them, and re-layouts  5.94 us (8%)
  between operations  1.32 us (2%)
    pallas_call x1, Pallas kernels, local(): pl.pallas_call(functools.partial(body, n_nodes=n_nodes, n_slab=n_slab), o...  67.4 us
    unnamed x16, local copies, waits for them, and re-layouts  5.94 us

profile of v2, /device:TPU:1, one launch (start us, length us, event | category | flops | bytes accessed | tf_op | source)
XLA Modules:
  0.0 74.6 jit_solution(3257885312799317836)
XLA Ops:
  1.3 0.0 copy-start.3
  1.3 0.0 copy-start.4
  1.3 0.0 copy-start.5
  1.3 0.7 copy-done.3
  2.0 0.0 copy-done.4
  2.0 0.0 copy-done.5
  2.0 0.0 copy-start
  2.0 1.2 %copy-done = s32[16,128,128]{2,1,0:T(8,128)S(1)} copy-done((s32[16,128,128]{2,1,0:T(8,128)S(1)}, s32[16,128,128]{2,1,0:T(8,128)}, u32[]{:S(2)}) %copy-start) | copy-done | bytes 1048600
  3.2 0.0 copy-start.1
  3.2 0.9 %copy-done.1 = bf16[64,1024]{1,0:T(8,128)(2,1)S(1)} copy-done((bf16[64,1024]{1,0:T(8,128)(2,1)S(1)}, bf16[64,1024]{1,0:T(8,128)(2,1)}, u32[]{:S(2)}) %copy-start.1) | copy-done | bytes 131096
  4.1 0.0 copy-start.2
  4.1 0.7 copy-done.2
  4.8 67.4 %gradient.1 = (f32[64,64]{1,0:T(8,128)S(1)}, f32[1,64]{1,0:T(1,128)S(1)}, f32[64,1024]{1,0:T(8,128)S(1)}, f32[1,1024]{1,0:T(1,128)S(1)}) custom-call(s32[2,16]{1,0:T(2,128)S(1)} %bitcast.9, f32[1,1]{1,0:T(1,128)} %bitcast.6.alpha_ref, bf16[1,64]{1,0:T(2,128)(2,1)S(1)} %bitcast.10, bf16[8,128]{1,0:T(8,128)(2,1)S(1)} %bitcast.8, bf16[64,64]{1,0:T(8,128)(2,1)S(1)} %copy-done.2, ...), custom_call_target="tpu_custom_call" | custom-call | tf_op jit(solution)/shard_map/gradient/pallas_call | solution.py:349
  72.2 0.6 copy.16
  72.8 0.5 copy.17
  73.3 0.7 copy.18
  74.0 0.6 copy.19
Async XLA Ops:
  1.3 0.7 copy-start.3
  1.3 0.7 copy-start.4
  1.3 0.7 copy-start.5
  2.0 1.2 %copy-start = (s32[16,128,128]{2,1,0:T(8,128)S(1)}, s32[16,128,128]{2,1,0:T(8,128)}, u32[]{:S(2)}) copy-start(s32[16,128,128]{2,1,0:T(8,128)} %counts_hbm.1) | copy-start | bytes 3145732
  3.2 0.9 %copy-start.1 = (bf16[64,1024]{1,0:T(8,128)(2,1)S(1)}, bf16[64,1024]{1,0:T(8,128)(2,1)}, u32[]{:S(2)}) copy-start(bf16[64,1024]{1,0:T(8,128)(2,1)} %npos_hbm.1) | copy-start | bytes 393220
  4.1 0.7 copy-start.2

commit v3 on v2

v3 whole, which is shorter than its diff:
```python
import functools

import jax
import jax.numpy as jnp
from jax import lax
from jax.experimental import pallas as pl
from jax.experimental.pallas import tpu as pltpu
from jax.sharding import PartitionSpec as P

MESH = pl.DeviceIdType.MESH
F32 = jnp.float32
BF16 = jnp.bfloat16
LOG2E = 1.4426950408889634
NX, NY, NZ = 4, 4, 8
XD = YD = (1, 3, 2)
XNEAR = (1, 3)
ZD = (1, 7, 2, 6, 3, 5, 4)
ORDER = (4, 3, 5, 2, 6, 7, 1, 0)
SLOT = {d: s for s, d in enumerate(ORDER)}
PB, QB = 512, 1024
TB = 128
KROWS = 80
VMEM_LIMIT = 56 * 1024 * 1024


def split3(v):
    a = v.astype(BF16).astype(F32)
    b = (v - a).astype(BF16).astype(F32)
    c = (v - a - b).astype(BF16).astype(F32)
    return a, b, c


def extras(scalars):
    a, b, c = split3(scalars)
    i = lax.broadcasted_iota(jnp.int32, (16, scalars.shape[1]), 0)
    one = jnp.where((i == 0) | (i == 4) | (i == 5), 1.0, 0.0)
    ext = jnp.where(i == 1, a, jnp.where(i == 2, b, jnp.where(i == 3, c, one)))
    return ext.astype(BF16)


def position():
    row, col = lax.axis_index("row"), lax.axis_index("col")
    return row // 2, row % 2, col % NY, col // NY


def enter(peers):
    barrier = pltpu.get_barrier_semaphore()
    for peer in peers:
        pl.semaphore_signal(barrier, inc=1, device_id=peer, device_id_type=MESH)
    pl.semaphore_wait(barrier, len(peers))


def all_peers():
    x, core, y, z = position()
    row, col = lax.axis_index("row"), lax.axis_index("col")
    xs = {d: {"row": (x + d) % NX * 2 + core, "col": col} for d in XD}
    sibling = {"row": x * 2 + 1 - core, "col": col}
    ys = {d: {"row": row, "col": z * NY + (y + d) % NY} for d in YD}
    zs = {d: {"row": row, "col": (z + d) % NZ * NY + y} for d in ZD}
    return xs, sibling, ys, zs


def remote(src, dst, ssem, rsem, peer):
    return pltpu.make_async_remote_copy(
        src_ref=src, dst_ref=dst, send_sem=ssem, recv_sem=rsem, device_id=peer, device_id_type=MESH
    )


def columns(ref, index, width):
    return ref.at[:, pl.ds(pl.multiple_of(index * width, 128), width)]


def params(**kw):
    return pltpu.CompilerParams(vmem_limit_bytes=VMEM_LIMIT, **kw)


def less(a, b):
    return jnp.minimum(jnp.maximum(b - a, 0), 1)


def same(a, b):
    return 1 - jnp.minimum((a - b) * (a - b), 1)


def body(
    blocks_hbm, alpha_hbm, sbias_hbm, nbias_hbm, spos_hbm, npos_hbm, counts_hbm,
    sg_ref, sb_ref, ng_ref, nb_ref,
    blocks_ref, alpha_ref, sbias_ref, nbias_ref, spos_ref, npos_ref, counts_ref, in_sem,
    order_ref, start_ref,
    s_ref, n_ref, nt_ref, st_ref, a_ref, racc, cacc, erow, ecol,
    ypiece, sib, xbuf, xin, zout, zin, yblk, yin,
    n_send, n_recv, f_send, f_recv, y_send, y_recv, z_send, z_recv,
    cf_send, cf_recv, cx_send, cx_recv, rz_send, rz_recv, ry_send, ry_recv,
    *, n_nodes, n_slab,
):
    x, core, y, z = position()
    xs, sibling, ys, zs = all_peers()
    width = npos_ref.shape[1]
    tiles = counts_ref.shape[0]
    copies = []

    def send(src, dst, ssem, rsem, peer):
        c = remote(src, dst, ssem, rsem, peer)
        c.start()
        copies.append(c)
        return c

    loads = [
        pltpu.make_async_copy(a, b, in_sem.at[i])
        for i, (a, b) in enumerate((
            (spos_hbm, spos_ref), (sbias_hbm, sbias_ref), (alpha_hbm, alpha_ref), (npos_hbm, npos_ref),
            (nbias_hbm, nbias_ref), (blocks_hbm, blocks_ref), (counts_hbm, counts_ref),
        ))
    ]
    for c in loads:
        c.start()
    enter([xs[d] for d in XD] + [sibling] + [ys[d] for d in YD] + [zs[d] for d in ZD])

    for c in loads[0:3]:
        c.wait()
    sp = spos_ref[...].astype(F32)
    u = LOG2E * (alpha_ref[0, 0] + sbias_ref[...].astype(F32) - jnp.sum(sp * sp, axis=0, keepdims=True))
    ypiece[y] = jnp.zeros((KROWS, 128), BF16)
    ypiece[y, 0:64, 0:64] = spos_ref[...]
    ypiece[y, 64:80, 0:64] = extras(u)
    yget = {d: send(ypiece.at[y], ypiece.at[y], y_send.at[d], y_recv.at[d], ys[d]) for d in YD}

    for c in loads[3:5]:
        c.wait()
    nodes = npos_ref[...].astype(F32)
    nb = nbias_ref[...].astype(F32)
    nb = jnp.concatenate([nb[i : i + 1] for i in range(width // 128)], axis=1)
    v = LOG2E * (nb - jnp.sum(nodes * nodes, axis=0, keepdims=True))
    mine = columns(n_ref, x * 2 + core, width)
    mine[0:64, :] = npos_ref[...]
    mine[64:80, :] = extras(v)
    for d in XNEAR:
        send(mine, mine, n_send.at[d], n_recv.at[d], xs[d])
    f0 = send(mine, mine, f_send.at[0], f_recv.at[0], sibling)

    def spans(n, f):
        def step(i, _):
            f(i)
            return 0

        lax.fori_loop(0, n, step, 0)

    for c in loads[5:7]:
        c.wait()

    def key(i, k):
        return blocks_ref[i, k] * tiles + k

    def ranks(k):
        for i in range(2):
            mykey = key(i, k)
            r = less(key(i, 0), mykey)
            for j in range(1, tiles):
                r += less(key(i, j), mykey)
            order_ref[2 + i, k] = r

    def orders(m):
        for i in range(2):
            r = 0
            for k in range(tiles):
                r += k * same(order_ref[2 + i, k], m)
            order_ref[i, m] = r

    def starts(t):
        for i in range(2):
            r = less(blocks_ref[i, 0], t)
            for k in range(1, tiles):
                r += less(blocks_ref[i, k], t)
            start_ref[i, t] = r

    racc[...] = jnp.zeros_like(racc)
    cacc[...] = jnp.zeros_like(cacc)
    spans(tiles, ranks)
    spans(tiles, orders)
    spans(start_ref.shape[1], starts)

    for d in YD:
        yget[d].wait_recv()
    lane = lax.broadcasted_iota(jnp.int32, (KROWS, 128), 1)
    own = s_ref.at[:, pl.ds(SLOT[0] * 256, 256)]
    for h in range(2):
        a, b = ypiece[2 * h].astype(F32), ypiece[2 * h + 1].astype(F32)
        own[:, h * 128 : h * 128 + 128] = jnp.where(lane < 64, a, pltpu.roll(b, 64, 1)).astype(BF16)
    zget = {}
    for d in ORDER[:-1]:
        dst = s_ref.at[:, pl.ds(SLOT[d] * 256, 256)]
        zget[d] = send(own, dst, z_send.at[d], z_recv.at[d], zs[d])

    def chip(d):
        return (x + d) % NX

    near, far = 1 + 2 * core, 3 - 2 * core

    def npiece(d, k):
        return columns(n_ref, chip(NX - d) * 2 + k, width)

    def npass(d):
        remote(npiece(d, core), npiece(d, core), n_send.at[d], n_recv.at[d], sibling).wait_recv()
        remote(npiece(d, core), npiece(d, core), f_send.at[d], f_recv.at[d], sibling).start()

    remote(npiece(near, core), npiece(near, core), n_send.at[near], n_recv.at[near], sibling).wait_recv()
    onward = {"row": chip(near) * 2 + core, "col": lax.axis_index("col")}
    send(npiece(near, core), npiece(near, core), n_send.at[2], n_recv.at[2], onward)
    remote(npiece(near, core), npiece(near, core), f_send.at[near], f_recv.at[near], sibling).start()
    npass(far)

    def prep_rows(slot):
        sl = pl.ds(slot * 256, 256)
        s = s_ref[:, sl].astype(F32)
        h1, h2, h3 = split3(s[0:64] * (2.0 * LOG2E))
        k = lax.broadcasted_iota(jnp.int32, (16, 256), 0)
        one = jnp.where((k >= 1) & (k <= 3), 1.0, 0.0)
        e = jnp.where(k == 0, s[65:66], jnp.where(k == 4, s[66:67], jnp.where(k == 5, s[67:68], one)))
        t = jnp.concatenate([h1, h2, h3, e, jnp.zeros((48, 256), F32)], axis=0)
        a_ref[sl, :] = t.T.astype(BF16)

    def prep_cols(j):
        n = columns(n_ref, j, width)[...]
        t = jnp.concatenate([n.astype(F32), jnp.zeros((48, width), F32)], axis=0).T.astype(BF16)
        nt_ref[pl.ds(j * (width // TB), width // TB)] = t.reshape(width // TB, TB, 128)

    def sweep(row, n_rows, column, n_cols):
        q = pl.ds(pl.multiple_of(column, 128), n_cols)
        sl = pl.ds(pl.multiple_of(row, 128), n_rows)
        n = n_ref[:, q]
        b = jnp.concatenate([n[0:64], n[0:64], n, jnp.zeros((48, n_cols), BF16)], axis=0)
        t = jnp.dot(a_ref[sl, :], b, preferred_element_type=F32)
        lam = jnp.exp2(t).astype(BF16)
        nt = nt_ref[pl.ds(column // TB, n_cols // TB)].reshape(n_cols, 128)
        racc[sl, :] -= jnp.dot(lam, nt, preferred_element_type=F32)
        cacc[:, q] -= jnp.dot(s_ref[:, sl], lam, preferred_element_type=F32)

    def pair(p, j):
        sweep(p * 512, 512, j * width, width)

    def single(slot, c):
        sweep(slot * 256, 256, c * (2 * width), 2 * width)

    prep_rows(SLOT[0])
    f0.wait_recv()
    prep_cols(x * 2)
    prep_cols(x * 2 + 1)

    def nready(d):
        remote(npiece(d, core), npiece(d, core), f_send.at[d], f_recv.at[d], sibling).wait_recv()

    def own_first(i):
        d = 1 + 2 * i - 3 * (i // 2)

        @pl.when(i == 0)
        def _():
            nready(1)
            nready(3)

        @pl.when(i == 2)
        def _():
            npass(2)
            nready(2)

        c = chip(NX - d)
        prep_cols(c * 2)
        prep_cols(c * 2 + 1)
        single(SLOT[0], c)

    spans(3, own_first)
    for d in XD:
        copies.append(remote(npiece(d, core), npiece(d, core), f_send.at[d], f_recv.at[d], sibling))

    for d in ORDER[0:2]:
        zget[d].wait_recv()
        prep_rows(SLOT[d])
    spans(8, lambda i: pair(0, (x * 2 + i) % 8))
    for d in ORDER[2:-1]:
        zget[d].wait_recv()
        prep_rows(SLOT[d])

    for d in ORDER:
        for h in range(2):
            st_ref[(z + NZ - d) % NZ * 2 + h] = s_ref[:, pl.ds(SLOT[d] * 256 + h * TB, TB)]
    erow[0] = jnp.zeros((TB, 128), F32)
    ecol[0] = jnp.zeros((KROWS, TB), F32)

    def edge(g):
        rsum, csum = erow[g * 4], ecol[g * 4]
        for i in range(4):
            m = g * 4 + i
            k = order_ref[0, m]
            yk = counts_ref[k].astype(F32).astype(BF16)
            rsum += jnp.dot(yk, nt_ref[blocks_ref[1, k]], preferred_element_type=F32)
            erow[m + 1] = rsum
            k = order_ref[1, m]
            yk = counts_ref[k].astype(F32).astype(BF16)
            csum += jnp.dot(st_ref[blocks_ref[0, k]], yk, preferred_element_type=F32)
            ecol[m + 1] = csum

    spans(tiles // 4, edge)

    def place_cols(g):
        for i in range(4):
            t = g * 4 + i
            cacc[:, pl.ds(pl.multiple_of(t * TB, TB), TB)] += ecol[start_ref[1, t + 1]] - ecol[start_ref[1, t]]

    spans(cacc.shape[1] // TB // 4, place_cols)

    def centred(sums, pos):
        return jnp.concatenate([sums[0:64] - pos[0:64].astype(F32) * sums[64:65], sums[64:80]], axis=0)

    def rows_done(slot):
        parts = []
        for h in range(2):
            t = (z + NZ - ORDER[slot]) % NZ * 2 + h
            acc = racc[pl.ds(slot * 256 + h * TB, TB), :]
            parts.append(acc + erow[start_ref[0, t + 1]] - erow[start_ref[0, t]])
        return centred(jnp.concatenate(parts, axis=0).T[0:KROWS], s_ref[:, pl.ds(slot * 256, 256)])

    rget = {}

    def rows_out(slot):
        e = (NZ - ORDER[slot]) % NZ
        zout[e] = rows_done(slot).astype(BF16)
        rget[e] = send(zout.at[e], zin.at[e], rz_send.at[e], rz_recv.at[e], zs[e])

    cget, xget = {}, {}

    def cols_other(d):
        src = columns(cacc, chip(d) * 2 + 1 - core, width)
        cget[d] = send(src, sib.at[d], cf_send.at[d], cf_recv.at[d], sibling)

    def cols_out(d):
        j = chip(d) * 2 + core
        cget[d].wait_recv()
        for h in range(width // 256):
            sl = pl.ds(h * 256, 256)
            sums = columns(cacc, j, width)[:, sl] + sib[d, :, sl]
            xbuf[d, :, sl] = centred(sums, columns(n_ref, j, width)[:, sl]).astype(BF16)
        xget[d] = send(xbuf.at[d], xin.at[d], cx_send.at[d], cx_recv.at[d], xs[d])

    def cols_of(d, first, n):
        single(6, chip(d))
        spans(n, lambda i: pair(first + i, chip(d) * 2 + 1 - core))
        cols_other(d)
        spans(n, lambda i: pair(first + i, chip(d) * 2 + core))
        cols_out(d)

    rows_out(0)
    rows_out(1)
    cols_of(2, 1, 2)
    spans(6, lambda i: pair(1, chip(3 + i // 2) * 2 + i % 2))
    rows_out(2)
    rows_out(3)
    cols_of(1, 2, 1)
    cols_of(3, 2, 1)
    spans(2, lambda i: pair(2, x * 2 + i))
    rows_out(4)
    rows_out(5)
    single(6, x)
    rows_out(6)
    single(7, x)
    cols_other(0)

    total = rows_done(7)
    for e in (4, 5, 3, 6, 2, 1, 7):
        rget[e].wait_recv()
        total += zin[e].astype(F32)
    yblk[0] = total[:, 0:128]
    yblk[1] = total[:, 128:256]
    yback = {d: send(yblk.at[(y + d) % NY // 2], yin.at[d], ry_send.at[d], ry_recv.at[d], ys[d]) for d in YD}

    cget[0].wait_recv()
    for d in XD:
        xget[d].wait_recv()
    for h in range(width // 256):
        sl = pl.ds(h * 256, 256)
        acc = centred(columns(cacc, x * 2 + core, width)[:, sl] + sib[0, :, sl], npos_ref[:, sl])
        for d in XD:
            acc += xin[d, :, sl].astype(F32)
        ng_ref[:, sl] = acc[0:64] * (2.0 / n_slab)
        nb_ref[:, sl] = acc[64:65] * (1.0 / n_slab)

    for d in YD:
        yback[d].wait_recv()
    own_sums = yblk[y // 2]
    for d in YD:
        own_sums += yin[d]
    odd = jnp.broadcast_to(y % 2, own_sums.shape) == 1
    own_sums = jnp.where(odd, pltpu.roll(own_sums, 64, 1), own_sums)[:, 0:64]
    sg_ref[...] = own_sums[0:64] * (2.0 / n_nodes)
    sb_ref[...] = own_sums[64:65] * (1.0 / n_nodes)
    for c in copies:
        c.wait_send()


def local(slab_pos, slab_bias, node_pos, node_bias, alpha, edge_counts, edge_blocks):
    vmem = pl.BlockSpec(memory_space=pltpu.VMEM)
    hbm = pl.BlockSpec(memory_space=pltpu.HBM)
    dma = pltpu.SemaphoreType.DMA
    own_rows, own_cols = slab_pos.shape[1], node_pos.shape[1]
    rows = own_rows * lax.axis_size("col")
    cols = own_cols * lax.axis_size("row")
    n_slab = rows * lax.axis_size("row")
    n_nodes = cols * lax.axis_size("col")
    tiles = edge_counts.shape[0]
    pieces = [pltpu.VMEM((NX, KROWS, own_cols), t) for t in (F32, BF16, BF16)]
    group = pltpu.VMEM((NZ, KROWS, 256), BF16)
    sg, sb, ng, nb = pl.pallas_call(
        functools.partial(body, n_nodes=n_nodes, n_slab=n_slab),
        out_shape=(
            jax.ShapeDtypeStruct((64, own_rows), F32), jax.ShapeDtypeStruct((1, own_rows), F32),
            jax.ShapeDtypeStruct((64, own_cols), F32), jax.ShapeDtypeStruct((1, own_cols), F32),
        ),
        in_specs=[hbm] * 7,
        out_specs=(vmem,) * 4,
        scratch_shapes=[
            pltpu.SMEM((2, tiles), jnp.int32), pltpu.SMEM((1, 1), F32), pltpu.VMEM((1, own_rows), BF16),
            pltpu.VMEM((own_cols // 128, 128), BF16), pltpu.VMEM(slab_pos.shape, BF16), pltpu.VMEM(node_pos.shape, BF16),
            pltpu.VMEM(edge_counts.shape, jnp.int32), dma((7,)),
            pltpu.SMEM((4, tiles), jnp.int32), pltpu.SMEM((2, cols // TB + 1), jnp.int32),
            pltpu.VMEM((KROWS, rows), BF16), pltpu.VMEM((KROWS, cols), BF16), pltpu.VMEM((cols // TB, TB, 128), BF16),
            pltpu.VMEM((rows // TB, KROWS, TB), BF16),
            pltpu.VMEM((rows, 256), BF16), pltpu.VMEM((rows, 128), F32), pltpu.VMEM((KROWS, cols), F32),
            pltpu.VMEM((tiles + 1, TB, 128), F32), pltpu.VMEM((tiles + 1, KROWS, TB), F32),
            pltpu.VMEM((NY, KROWS, 128), BF16), *pieces, group, group,
            pltpu.VMEM((2, KROWS, 128), F32), pltpu.VMEM((NY, KROWS, 128), F32),
        ] + [dma((NX,))] * 4 + [dma((NY,))] * 2 + [dma((NZ,))] * 2
        + [dma((NX,))] * 4 + [dma((NZ,))] * 2 + [dma((NY,))] * 2,
        compiler_params=params(collective_id=0, has_side_effects=True),
        name="gradient",
    )(
        edge_blocks.T, alpha.reshape(1, 1), slab_bias.reshape(1, own_rows), node_bias.reshape(own_cols // 128, 128),
        slab_pos, node_pos, edge_counts,
    )
    return sg, sb.reshape(own_rows), ng, nb.reshape(own_cols)


def solution(mesh):
    in_specs = (
        P(None, ("row", "col")),
        P(("row", "col")),
        P(None, ("col", "row")),
        P(("col", "row")),
        P(),
        P(("row", "col"), None, None),
        P(("row", "col"), None),
    )
    out_specs = (
        P(None, ("row", "col")),
        P(("row", "col")),
        P(None, ("col", "row")),
        P(("col", "row")),
    )
    return jax.shard_map(local, mesh=mesh, in_specs=in_specs, out_specs=out_specs, check_vma=False)
```

time: 74.9 us -> 68.4 us (0.913)
  Pallas kernels: 67.4 us -> 62.2 us
  local copies, waits for them, and re-layouts: 5.94 us -> 4.16 us
    pallas_call x1, Pallas kernels: 67.4 us -> 62.2 us  [local(): pl.pallas_call(functools.partial(body, n_nodes=n_nodes, n_slab=n_slab), o...]
    unnamed x16 -> x8, local copies, waits for them, and re-layouts: 5.94 us -> 4.16 us
where the time goes in v3:
time: 68.4 us; the launch traced here: 67.7 us
  Pallas kernels  62.2 us (91%)
  local copies, waits for them, and re-layouts  4.16 us (6%)
  between operations  1.3 us (2%)
    pallas_call x1, Pallas kernels, local(): pl.pallas_call(functools.partial(body, n_nodes=n_nodes, n_slab=n_slab), o...  62.2 us
    unnamed x8, local copies, waits for them, and re-layouts  4.16 us

profile of v3, /device:TPU:1, one launch (start us, length us, event | category | flops | bytes accessed | tf_op | source)
XLA Modules:
  0.0 67.7 jit_solution(5621701587790240311)
XLA Ops:
  1.3 62.2 %gradient.1 = (f32[64,64]{1,0:T(8,128)}, f32[1,64]{1,0:T(1,128)}, f32[64,1024]{1,0:T(8,128)}, f32[1,1024]{1,0:T(1,128)}) custom-call(s32[2,16]{1,0:T(2,128)} %bitcast.9, f32[1,1]{1,0:T(1,128)} %bitcast.6.alpha_hbm, bf16[1,64]{1,0:T(2,128)(2,1)} %bitcast.10, bf16[8,128]{1,0:T(8,128)(2,1)} %bitcast.8, bf16[64,64]{1,0:T(8,128)(2,1)} %spos_hbm.1, ...), custom_call_target="tpu_custom_call" | custom-call | tf_op jit(solution)/shard_map/gradient/pallas_call | solution.py:410
  63.5 0.0 copy-start.1
  63.5 1.4 %copy.16 = f32[64,64]{1,0:T(8,128)} copy(f32[64,64]{1,0:T(8,128)} %get-tuple-element.16) | data formatting | bytes 32768
  64.9 0.0 copy-done.1
  64.9 0.5 copy.17
  65.4 0.0 copy-start
  65.4 1.7 %copy.18 = f32[64,1024]{1,0:T(8,128)} copy(f32[64,1024]{1,0:T(8,128)} %get-tuple-element.18) | data formatting | bytes 524288
  67.1 0.0 copy-done
  67.1 0.6 copy.19
Async XLA Ops:
  63.5 1.4 %copy-start.1 = (f32[1,64]{1,0:T(1,128)S(1)}, f32[1,64]{1,0:T(1,128)}, u32[]{:S(2)}) copy-start(f32[1,64]{1,0:T(1,128)} %get-tuple-element.9) | copy-start | bytes 772
  65.4 1.7 %copy-start = (f32[1,1024]{1,0:T(1,128)S(1)}, f32[1,1024]{1,0:T(1,128)}, u32[]{:S(2)}) copy-start(f32[1,1024]{1,0:T(1,128)} %get-tuple-element.11) | copy-start | bytes 12292

commit v4 on v3

--- a/solution.py
+++ b/solution.py
@@ -15,11 +15,15 @@
 XD = YD = (1, 3, 2)
 XNEAR = (1, 3)
 ZD = (1, 7, 2, 6, 3, 5, 4)
-ORDER = (4, 3, 5, 2, 6, 7, 1, 0)
+ORDER = (2, 6, 3, 5, 1, 7, 4, 0)
+ZSEND = (2, 6, 3, 5, 4, 1, 7)
+LATE = (1, 7)
+PIECE = 40
 SLOT = {d: s for s, d in enumerate(ORDER)}
-PB, QB = 512, 1024
+
 TB = 128
 KROWS = 80
+OROWS = 72
 VMEM_LIMIT = 56 * 1024 * 1024
 
 
@@ -74,24 +78,19 @@
     return pltpu.CompilerParams(vmem_limit_bytes=VMEM_LIMIT, **kw)
 
 
-def less(a, b):
-    return jnp.minimum(jnp.maximum(b - a, 0), 1)
-
-
-def same(a, b):
-    return 1 - jnp.minimum((a - b) * (a - b), 1)
+def below(a, b):
+    return lax.shift_right_arithmetic(a - b, 31)
 
 
 def body(
     blocks_hbm, alpha_hbm, sbias_hbm, nbias_hbm, spos_hbm, npos_hbm, counts_hbm,
-    sg_ref, sb_ref, ng_ref, nb_ref,
+    rout_ref, cout_ref,
     blocks_ref, alpha_ref, sbias_ref, nbias_ref, spos_ref, npos_ref, counts_ref, in_sem,
     order_ref, start_ref,
     s_ref, n_ref, nt_ref, st_ref, a_ref, racc, cacc, erow, ecol,
-    ypiece, sib, xbuf, xin, zout, zin, yblk, yin,
+    ypiece, sib, xbuf, xin, zout, zin, lout, lin, yblk, yin,
     n_send, n_recv, f_send, f_recv, y_send, y_recv, z_send, z_recv,
-    cf_send, cf_recv, cx_send, cx_recv, rz_send, rz_recv, ry_send, ry_recv,
-    *, n_nodes, n_slab,
+    cf_send, cf_recv, cx_send, cx_recv, rz_send, rz_recv, l_send, l_recv, ry_send, ry_recv,
 ):
     x, core, y, z = position()
     xs, sibling, ys, zs = all_peers()
@@ -114,7 +113,10 @@
     ]
     for c in loads:
         c.start()
-    enter([xs[d] for d in XD] + [sibling] + [ys[d] for d in YD] + [zs[d] for d in ZD])
+    corners = [
+        {"row": lax.axis_index("row"), "col": (z + e) % NZ * NY + (y + d) % NY} for e in LATE for d in YD
+    ]
+    enter([xs[d] for d in XD] + [sibling] + [ys[d] for d in YD] + [zs[d] for d in ZD] + corners)
 
     for c in loads[0:3]:
         c.wait()
@@ -148,36 +150,40 @@
     for c in loads[5:7]:
         c.wait()
 
-    def key(i, k):
-        return blocks_ref[i, k] * tiles + k
-
-    def ranks(k):
-        for i in range(2):
-            mykey = key(i, k)
-            r = less(key(i, 0), mykey)
-            for j in range(1, tiles):
-                r += less(key(i, j), mykey)
-            order_ref[2 + i, k] = r
-
-    def orders(m):
-        for i in range(2):
+    def sort(i, n_blocks):
+        block = [blocks_ref[i, k] for k in range(tiles)]
+        keys = [b * tiles + k for k, b in enumerate(block)]
+        rank = [jnp.int32(k) for k in range(tiles)]
+        for k in range(tiles):
+            for j in range(k):
+                r = 1 + below(keys[j], keys[k])
+                rank[k] = rank[k] - r
+                rank[j] = rank[j] + r
+
+        for k in range(tiles):
+            order_ref[2 + i, k] = rank[k]
+
+        def orders(m):
             r = 0
-            for k in range(tiles):
-                r += k * same(order_ref[2 + i, k], m)
+            for k in range(1, tiles):
+                d = order_ref[2 + i, k] - m
+                r += k - k * jnp.minimum(d * d, 1)
             order_ref[i, m] = r
 
-    def starts(t):
-        for i in range(2):
-            r = less(blocks_ref[i, 0], t)
-            for k in range(1, tiles):
-                r += less(blocks_ref[i, k], t)
+        spans(tiles, orders)
+
+        def starts(t):
+            r = 0
+            for b in block:
+                r -= below(b, t)
             start_ref[i, t] = r
+
+        spans(n_blocks + 1, starts)
 
     racc[...] = jnp.zeros_like(racc)
     cacc[...] = jnp.zeros_like(cacc)
-    spans(tiles, ranks)
-    spans(tiles, orders)
-    spans(start_ref.shape[1], starts)
+    sort(0, racc.shape[0] // TB)
+    sort(1, cacc.shape[1] // TB)
 
     for d in YD:
         yget[d].wait_recv()
@@ -187,7 +193,7 @@
         a, b = ypiece[2 * h].astype(F32), ypiece[2 * h + 1].astype(F32)
         own[:, h * 128 : h * 128 + 128] = jnp.where(lane < 64, a, pltpu.roll(b, 64, 1)).astype(BF16)
     zget = {}
-    for d in ORDER[:-1]:
+    for d in ZSEND:
         dst = s_ref.at[:, pl.ds(SLOT[d] * 256, 256)]
         zget[d] = send(own, dst, z_send.at[d], z_recv.at[d], zs[d])
 
@@ -202,12 +208,6 @@
     def npass(d):
         remote(npiece(d, core), npiece(d, core), n_send.at[d], n_recv.at[d], sibling).wait_recv()
         remote(npiece(d, core), npiece(d, core), f_send.at[d], f_recv.at[d], sibling).start()
-
-    remote(npiece(near, core), npiece(near, core), n_send.at[near], n_recv.at[near], sibling).wait_recv()
-    onward = {"row": chip(near) * 2 + core, "col": lax.axis_index("col")}
-    send(npiece(near, core), npiece(near, core), n_send.at[2], n_recv.at[2], onward)
-    remote(npiece(near, core), npiece(near, core), f_send.at[near], f_recv.at[near], sibling).start()
-    npass(far)
 
     def prep_rows(slot):
         sl = pl.ds(slot * 256, 256)
@@ -245,36 +245,39 @@
     f0.wait_recv()
     prep_cols(x * 2)
     prep_cols(x * 2 + 1)
+    single(SLOT[0], x)
+    remote(npiece(near, core), npiece(near, core), n_send.at[near], n_recv.at[near], sibling).wait_recv()
+    onward = {"row": chip(near) * 2 + core, "col": lax.axis_index("col")}
+    send(npiece(near, core), npiece(near, core), n_send.at[2], n_recv.at[2], onward)
+    remote(npiece(near, core), npiece(near, core), f_send.at[near], f_recv.at[near], sibling).start()
+    npass(far)
+
 
     def nready(d):
         remote(npiece(d, core), npiece(d, core), f_send.at[d], f_recv.at[d], sibling).wait_recv()
 
-    def own_first(i):
-        d = 1 + 2 * i - 3 * (i // 2)
-
-        @pl.when(i == 0)
-        def _():
-            nready(1)
-            nready(3)
-
-        @pl.when(i == 2)
-        def _():
-            npass(2)
-            nready(2)
-
+    def own_near(i):
+        d = 1 + 2 * i
+        nready(d)
         c = chip(NX - d)
         prep_cols(c * 2)
         prep_cols(c * 2 + 1)
         single(SLOT[0], c)
 
-    spans(3, own_first)
-    for d in XD:
-        copies.append(remote(npiece(d, core), npiece(d, core), f_send.at[d], f_recv.at[d], sibling))
-
+    spans(2, own_near)
     for d in ORDER[0:2]:
         zget[d].wait_recv()
         prep_rows(SLOT[d])
-    spans(8, lambda i: pair(0, (x * 2 + i) % 8))
+    spans(2, lambda i: pair(0, x * 2 + i))
+    npass(2)
+    spans(4, lambda i: pair(0, chip(3 + i // 2 * 2) * 2 + i % 2))
+    nready(2)
+    for d in XD:
+        copies.append(remote(npiece(d, core), npiece(d, core), f_send.at[d], f_recv.at[d], sibling))
+    prep_cols(chip(2) * 2)
+    prep_cols(chip(2) * 2 + 1)
+    single(SLOT[0], chip(2))
+    spans(2, lambda i: pair(0, chip(2) * 2 + i))
     for d in ORDER[2:-1]:
         zget[d].wait_recv()
         prep_rows(SLOT[d])
@@ -325,74 +328,110 @@
         zout[e] = rows_done(slot).astype(BF16)
         rget[e] = send(zout.at[e], zin.at[e], rz_send.at[e], rz_recv.at[e], zs[e])
 
+    def pack(block):
+        lane = lax.broadcasted_iota(jnp.int32, (PIECE, 128), 1)
+        out = []
+        for h in range(2):
+            top, low = block[0:PIECE, h * 128 : h * 128 + 128], block[PIECE:KROWS, h * 128 : h * 128 + 128]
+            out.append(jnp.where(lane < 64, top, pltpu.roll(low, 64, 1)))
+            out.append(jnp.where(lane < 64, pltpu.roll(top, 64, 1), low))
+        return out
+
+    late = {}
+
+    def rows_late(i):
+        e = NZ - LATE[i]
+        for t, p in enumerate(pack(rows_done(SLOT[LATE[i]]))):
+            lout[i, t] = p
+        for d in range(NY):
+            peer = {"row": lax.axis_index("row"), "col": (z + e) % NZ * NY + (y + d) % NY}
+            late[i, d] = send(lout.at[i, (y + d) % NY], lin.at[i, d], l_send.at[i, d], l_recv.at[i, d], peer)
+
     cget, xget = {}, {}
 
     def cols_other(d):
-        src = columns(cacc, chip(d) * 2 + 1 - core, width)
+        src = columns(cacc, chip(d) * 2 + 1 - core, width).at[0:OROWS]
         cget[d] = send(src, sib.at[d], cf_send.at[d], cf_recv.at[d], sibling)
 
+    def cols_sum(d):
+        cget[d].wait_recv()
+        xbuf[d] = columns(cacc, chip(d) * 2 + core, width)[0:OROWS] + sib[d]
+
     def cols_out(d):
-        j = chip(d) * 2 + core
-        cget[d].wait_recv()
-        for h in range(width // 256):
-            sl = pl.ds(h * 256, 256)
-            sums = columns(cacc, j, width)[:, sl] + sib[d, :, sl]
-            xbuf[d, :, sl] = centred(sums, columns(n_ref, j, width)[:, sl]).astype(BF16)
+        cols_sum(d)
+
+        @pl.when(near == d)
+        def _():
+            relayed.wait_recv()
+            xbuf[d] += xin[2]
+
         xget[d] = send(xbuf.at[d], xin.at[d], cx_send.at[d], cx_recv.at[d], xs[d])
 
-    def cols_of(d, first, n):
-        single(6, chip(d))
-        spans(n, lambda i: pair(first + i, chip(d) * 2 + 1 - core))
-        cols_other(d)
-        spans(n, lambda i: pair(first + i, chip(d) * 2 + core))
-        cols_out(d)
+    def cols_units(d, first, n, k):
+        spans(n, lambda i: pair(first + i, chip(d) * 2 + k))
 
     rows_out(0)
     rows_out(1)
-    cols_of(2, 1, 2)
+    single(6, chip(2))
+    cols_units(2, 1, 2, 1 - core)
+    cols_other(2)
+    cols_units(2, 1, 2, core)
+    cols_sum(2)
+    relayed = send(xbuf.at[2], xin.at[2], cx_send.at[2], cx_recv.at[2], onward)
+    spans(3, lambda i: single(6, chip(3 + i)))
+    rows_out(6)
     spans(6, lambda i: pair(1, chip(3 + i // 2) * 2 + i % 2))
     rows_out(2)
     rows_out(3)
-    cols_of(1, 2, 1)
-    cols_of(3, 2, 1)
-    spans(2, lambda i: pair(2, x * 2 + i))
-    rows_out(4)
-    rows_out(5)
-    single(6, x)
-    rows_out(6)
-    single(7, x)
+    for d in XNEAR:
+        cols_units(d, 2, 1, 1 - core)
+        cols_other(d)
+        cols_units(d, 2, 1, core)
+        cols_out(d)
+    cols_units(0, 2, 1, 1 - core)
     cols_other(0)
+    cols_units(0, 2, 1, core)
+    rows_late(0)
+    rows_late(1)
 
     total = rows_done(7)
-    for e in (4, 5, 3, 6, 2, 1, 7):
+    for e in (6, 2, 4, 5, 3):
         rget[e].wait_recv()
         total += zin[e].astype(F32)
-    yblk[0] = total[:, 0:128]
-    yblk[1] = total[:, 128:256]
-    yback = {d: send(yblk.at[(y + d) % NY // 2], yin.at[d], ry_send.at[d], ry_recv.at[d], ys[d]) for d in YD}
+    for t, p in enumerate(pack(total)):
+        yblk[t] = p
+    yback = {d: send(yblk.at[(y + d) % NY], yin.at[d], ry_send.at[d], ry_recv.at[d], ys[d]) for d in YD}
 
     cget[0].wait_recv()
-    for d in XD:
+    for d in XNEAR:
         xget[d].wait_recv()
     for h in range(width // 256):
         sl = pl.ds(h * 256, 256)
-        acc = centred(columns(cacc, x * 2 + core, width)[:, sl] + sib[0, :, sl], npos_ref[:, sl])
-        for d in XD:
-            acc += xin[d, :, sl].astype(F32)
-        ng_ref[:, sl] = acc[0:64] * (2.0 / n_slab)
-        nb_ref[:, sl] = acc[64:65] * (1.0 / n_slab)
-
+        acc = columns(cacc, x * 2 + core, width)[0:OROWS, sl] + sib[0, :, sl]
+        acc += xin[1, :, sl] + xin[3, :, sl]
+        cout_ref[:, sl] = acc
+
+    own_sums = yblk[y]
+    for key in late:
+        late[key].wait_recv()
+        own_sums += lin[key]
     for d in YD:
         yback[d].wait_recv()
-    own_sums = yblk[y // 2]
-    for d in YD:
         own_sums += yin[d]
-    odd = jnp.broadcast_to(y % 2, own_sums.shape) == 1
-    own_sums = jnp.where(odd, pltpu.roll(own_sums, 64, 1), own_sums)[:, 0:64]
-    sg_ref[...] = own_sums[0:64] * (2.0 / n_nodes)
-    sb_ref[...] = own_sums[64:65] * (1.0 / n_nodes)
+    rout_ref[...] = own_sums
     for c in copies:
         c.wait_send()
+
+
+def finish(npos_ref, rows_ref, cols_ref, sg_ref, sb_ref, ng_ref, nb_ref, *, n_nodes, n_slab):
+    r = rows_ref[...]
+    low = pltpu.roll(r, 64, 1)
+    sums = jnp.concatenate([r, low], axis=0)[:, 0:64]
+    sg_ref[...] = sums[0:64] * (2.0 / n_nodes)
+    sb_ref[...] = sums[64:65] * (1.0 / n_nodes)
+    tot = cols_ref[64:65, :]
+    ng_ref[...] = (cols_ref[0:64, :] - npos_ref[...].astype(F32) * tot) * (2.0 / n_slab)
+    nb_ref[...] = tot * (1.0 / n_slab)
 
 
 def local(slab_pos, slab_bias, node_pos, node_bias, alpha, edge_counts, edge_blocks):
@@ -405,16 +444,13 @@
     n_slab = rows * lax.axis_size("row")
     n_nodes = cols * lax.axis_size("col")
     tiles = edge_counts.shape[0]
-    pieces = [pltpu.VMEM((NX, KROWS, own_cols), t) for t in (F32, BF16, BF16)]
+    pieces = [pltpu.VMEM((NX, OROWS, own_cols), F32)] * 3
     group = pltpu.VMEM((NZ, KROWS, 256), BF16)
-    sg, sb, ng, nb = pl.pallas_call(
-        functools.partial(body, n_nodes=n_nodes, n_slab=n_slab),
-        out_shape=(
-            jax.ShapeDtypeStruct((64, own_rows), F32), jax.ShapeDtypeStruct((1, own_rows), F32),
-            jax.ShapeDtypeStruct((64, own_cols), F32), jax.ShapeDtypeStruct((1, own_cols), F32),
-        ),
+    row_sums, col_sums = pl.pallas_call(
+        body,
+        out_shape=(jax.ShapeDtypeStruct((PIECE, 128), F32), jax.ShapeDtypeStruct((OROWS, own_cols), F32)),
         in_specs=[hbm] * 7,
-        out_specs=(vmem,) * 4,
+        out_specs=(vmem,) * 2,
         scratch_shapes=[
             pltpu.SMEM((2, tiles), jnp.int32), pltpu.SMEM((1, 1), F32), pltpu.VMEM((1, own_rows), BF16),
             pltpu.VMEM((own_cols // 128, 128), BF16), pltpu.VMEM(slab_pos.shape, BF16), pltpu.VMEM(node_pos.shape, BF16),
@@ -425,15 +461,27 @@
             pltpu.VMEM((rows, 256), BF16), pltpu.VMEM((rows, 128), F32), pltpu.VMEM((KROWS, cols), F32),
             pltpu.VMEM((tiles + 1, TB, 128), F32), pltpu.VMEM((tiles + 1, KROWS, TB), F32),
             pltpu.VMEM((NY, KROWS, 128), BF16), *pieces, group, group,
-            pltpu.VMEM((2, KROWS, 128), F32), pltpu.VMEM((NY, KROWS, 128), F32),
+            pltpu.VMEM((2, NY, PIECE, 128), F32), pltpu.VMEM((2, NY, PIECE, 128), F32),
+            pltpu.VMEM((NY, PIECE, 128), F32), pltpu.VMEM((NY, PIECE, 128), F32),
         ] + [dma((NX,))] * 4 + [dma((NY,))] * 2 + [dma((NZ,))] * 2
-        + [dma((NX,))] * 4 + [dma((NZ,))] * 2 + [dma((NY,))] * 2,
+        + [dma((NX,))] * 4 + [dma((NZ,))] * 2 + [dma((2, NY))] * 2 + [dma((NY,))] * 2,
         compiler_params=params(collective_id=0, has_side_effects=True),
         name="gradient",
     )(
         edge_blocks.T, alpha.reshape(1, 1), slab_bias.reshape(1, own_rows), node_bias.reshape(own_cols // 128, 128),
         slab_pos, node_pos, edge_counts,
     )
+    sg, sb, ng, nb = pl.pallas_call(
+        functools.partial(finish, n_nodes=n_nodes, n_slab=n_slab),
+        out_shape=(
+            jax.ShapeDtypeStruct((64, own_rows), F32), jax.ShapeDtypeStruct((1, own_rows), F32),
+            jax.ShapeDtypeStruct((64, own_cols), F32), jax.ShapeDtypeStruct((1, own_cols), F32),
+        ),
+        in_specs=[vmem] * 3,
+        out_specs=(vmem,) * 4,
+        compiler_params=params(),
+        name="finish",
+    )(node_pos, row_sums, col_sums)
     return sg, sb.reshape(own_rows), ng, nb.reshape(own_cols)
 
 

time: 68.4 us -> 60.8 us (0.89)
  local copies, waits for them, and re-layouts: 4.16 us -> 0 us
  Pallas kernels: 62.2 us -> 59.4 us
    unnamed x8 -> x0, local copies, waits for them, and re-layouts: 4.16 us -> none
    pallas_call x1 -> x2, Pallas kernels: 62.2 us -> 59.4 us  [the longest x1 57.6 us: local(): pl.pallas_call(body, out_shape=(jax.ShapeDtypeStruct((PIECE, 128), F32),...]
where the time goes in v4:
time: 60.8 us; the launch traced here: 60.7 us
  Pallas kernels  59.4 us (98%)
  between operations  1.29 us (2%)
    pallas_call x1, Pallas kernels, local(): pl.pallas_call(body, out_shape=(jax.ShapeDtypeStruct((PIECE, 128), F32),...  57.6 us
    pallas_call x1, Pallas kernels, local(): pl.pallas_call(functools.partial(finish, n_nodes=n_nodes, n_slab=n_slab),...  1.83 us

profile of v4, /device:TPU:1, one launch (start us, length us, event | category | flops | bytes accessed | tf_op | source)
XLA Modules:
  0.0 60.7 jit_solution(14023346530135764695)
XLA Ops:
  1.3 57.6 %gradient.1 = (f32[40,128]{1,0:T(8,128)}, f32[72,1024]{1,0:T(8,128)}) custom-call(s32[2,16]{1,0:T(2,128)} %bitcast.8, f32[1,1]{1,0:T(1,128)} %bitcast.6.alpha_hbm, bf16[1,64]{1,0:T(2,128)(2,1)} %bitcast.9, bf16[8,128]{1,0:T(8,128)(2,1)} %bitcast.7, bf16[64,64]{1,0:T(8,128)(2,1)} %spos_hbm.1, bf16[64,1024]{1,0:T(8,128)(2,1)} %npos_ref.1, ...), custom_call_target="tpu_custom_call" | custom-call | tf_op jit(solution)/shard_map/gradient/pallas_call | solution.py:449
  58.9 1.8 %finish.1 = (f32[64,64]{1,0:T(8,128)}, f32[1,64]{1,0:T(1,128)}, f32[64,1024]{1,0:T(8,128)}, f32[1,1024]{1,0:T(1,128)}) custom-call(bf16[64,1024]{1,0:T(8,128)(2,1)} %npos_ref.1, f32[40,128]{1,0:T(8,128)} %get-tuple-element.10.rows_ref, f32[72,1024]{1,0:T(8,128)} %get-tuple-element.11.cols_ref), custom_call_target="tpu_custom_call" | custom-call | tf_op jit(solution)/shard_map/finish/pallas_call | solution.py:474

commit v5 on v4

--- a/solution.py
+++ b/solution.py
@@ -47,11 +47,9 @@
     return row // 2, row % 2, col % NY, col // NY
 
 
-def enter(peers):
-    barrier = pltpu.get_barrier_semaphore()
+def greet(peers):
     for peer in peers:
-        pl.semaphore_signal(barrier, inc=1, device_id=peer, device_id_type=MESH)
-    pl.semaphore_wait(barrier, len(peers))
+        pl.semaphore_signal(pltpu.get_barrier_semaphore(), inc=1, device_id=peer, device_id_type=MESH)
 
 
 def all_peers():
@@ -78,15 +76,27 @@
     return pltpu.CompilerParams(vmem_limit_bytes=VMEM_LIMIT, **kw)
 
 
-def below(a, b):
-    return lax.shift_right_arithmetic(a - b, 31)
+def tile_tables(keys, tiles):
+    lane = lax.broadcasted_iota(jnp.int32, (tiles, 128), 1)
+    tile = lax.broadcasted_iota(jnp.int32, (tiles, 128), 0)
+    column = keys.T
+    orders, starts = [], []
+    for i in range(2):
+        k = jnp.broadcast_to(column[0:tiles, i : i + 1], (tiles, 128))
+        j = jnp.broadcast_to(keys[i : i + 1, :], (tiles, 128))
+        before = jnp.where((lane < tiles) & ((j < k) | ((j == k) & (lane < tile))), 1, 0)
+        rank = jnp.broadcast_to(jnp.sum(before, axis=1, keepdims=True), (tiles, 128))
+        here = jnp.where(rank == lane, tile, 0)
+        orders.append(jnp.sum(here, axis=0, keepdims=True))
+        starts.append(jnp.sum(jnp.where(k < lane, 1, 0), axis=0, keepdims=True))
+    return jnp.concatenate(orders + starts + [jnp.zeros((4, 128), jnp.int32)], axis=0)
 
 
 def body(
     blocks_hbm, alpha_hbm, sbias_hbm, nbias_hbm, spos_hbm, npos_hbm, counts_hbm,
     rout_ref, cout_ref,
     blocks_ref, alpha_ref, sbias_ref, nbias_ref, spos_ref, npos_ref, counts_ref, in_sem,
-    order_ref, start_ref,
+    bvec_ref, table_ref, order_ref,
     s_ref, n_ref, nt_ref, st_ref, a_ref, racc, cacc, erow, ecol,
     ypiece, sib, xbuf, xin, zout, zin, lout, lin, yblk, yin,
     n_send, n_recv, f_send, f_recv, y_send, y_recv, z_send, z_recv,
@@ -108,7 +118,8 @@
         pltpu.make_async_copy(a, b, in_sem.at[i])
         for i, (a, b) in enumerate((
             (spos_hbm, spos_ref), (sbias_hbm, sbias_ref), (alpha_hbm, alpha_ref), (npos_hbm, npos_ref),
-            (nbias_hbm, nbias_ref), (blocks_hbm, blocks_ref), (counts_hbm, counts_ref),
+            (nbias_hbm, nbias_ref), (blocks_hbm, blocks_ref),
+            (blocks_hbm, bvec_ref), (counts_hbm, counts_ref),
         ))
     ]
     for c in loads:
@@ -116,7 +127,8 @@
     corners = [
         {"row": lax.axis_index("row"), "col": (z + e) % NZ * NY + (y + d) % NY} for e in LATE for d in YD
     ]
-    enter([xs[d] for d in XD] + [sibling] + [ys[d] for d in YD] + [zs[d] for d in ZD] + corners)
+    peers = [xs[d] for d in XD] + [sibling] + [ys[d] for d in YD] + [zs[d] for d in ZD] + corners
+    greet(peers)
 
     for c in loads[0:3]:
         c.wait()
@@ -125,7 +137,6 @@
     ypiece[y] = jnp.zeros((KROWS, 128), BF16)
     ypiece[y, 0:64, 0:64] = spos_ref[...]
     ypiece[y, 64:80, 0:64] = extras(u)
-    yget = {d: send(ypiece.at[y], ypiece.at[y], y_send.at[d], y_recv.at[d], ys[d]) for d in YD}
 
     for c in loads[3:5]:
         c.wait()
@@ -136,6 +147,8 @@
     mine = columns(n_ref, x * 2 + core, width)
     mine[0:64, :] = npos_ref[...]
     mine[64:80, :] = extras(v)
+    pl.semaphore_wait(pltpu.get_barrier_semaphore(), len(peers))
+    yget = {d: send(ypiece.at[y], ypiece.at[y], y_send.at[d], y_recv.at[d], ys[d]) for d in YD}
     for d in XNEAR:
         send(mine, mine, n_send.at[d], n_recv.at[d], xs[d])
     f0 = send(mine, mine, f_send.at[0], f_recv.at[0], sibling)
@@ -147,43 +160,16 @@
 
         lax.fori_loop(0, n, step, 0)
 
-    for c in loads[5:7]:
+    for c in loads[5:8]:
         c.wait()
-
-    def sort(i, n_blocks):
-        block = [blocks_ref[i, k] for k in range(tiles)]
-        keys = [b * tiles + k for k, b in enumerate(block)]
-        rank = [jnp.int32(k) for k in range(tiles)]
-        for k in range(tiles):
-            for j in range(k):
-                r = 1 + below(keys[j], keys[k])
-                rank[k] = rank[k] - r
-                rank[j] = rank[j] + r
-
-        for k in range(tiles):
-            order_ref[2 + i, k] = rank[k]
-
-        def orders(m):
-            r = 0
-            for k in range(1, tiles):
-                d = order_ref[2 + i, k] - m
-                r += k - k * jnp.minimum(d * d, 1)
-            order_ref[i, m] = r
-
-        spans(tiles, orders)
-
-        def starts(t):
-            r = 0
-            for b in block:
-                r -= below(b, t)
-            start_ref[i, t] = r
-
-        spans(n_blocks + 1, starts)
 
     racc[...] = jnp.zeros_like(racc)
     cacc[...] = jnp.zeros_like(cacc)
-    sort(0, racc.shape[0] // TB)
-    sort(1, cacc.shape[1] // TB)
+    table_ref[...] = jnp.zeros_like(table_ref)
+    table_ref[0:2, 0:tiles] = bvec_ref[...]
+    table_ref[...] = tile_tables(table_ref[...], tiles)
+    tables = pltpu.make_async_copy(table_ref, order_ref, in_sem.at[8])
+    tables.start()
 
     for d in YD:
         yget[d].wait_recv()
@@ -217,11 +203,11 @@
         one = jnp.where((k >= 1) & (k <= 3), 1.0, 0.0)
         e = jnp.where(k == 0, s[65:66], jnp.where(k == 4, s[66:67], jnp.where(k == 5, s[67:68], one)))
         t = jnp.concatenate([h1, h2, h3, e, jnp.zeros((48, 256), F32)], axis=0)
-        a_ref[sl, :] = t.T.astype(BF16)
+        a_ref[sl, :] = t.astype(BF16).T
 
     def prep_cols(j):
         n = columns(n_ref, j, width)[...]
-        t = jnp.concatenate([n.astype(F32), jnp.zeros((48, width), F32)], axis=0).T.astype(BF16)
+        t = jnp.concatenate([n, jnp.zeros((48, width), BF16)], axis=0).T
         nt_ref[pl.ds(j * (width // TB), width // TB)] = t.reshape(width // TB, TB, 128)
 
     def sweep(row, n_rows, column, n_cols):
@@ -285,18 +271,22 @@
     for d in ORDER:
         for h in range(2):
             st_ref[(z + NZ - d) % NZ * 2 + h] = s_ref[:, pl.ds(SLOT[d] * 256 + h * TB, TB)]
+    tables.wait()
     erow[0] = jnp.zeros((TB, 128), F32)
     ecol[0] = jnp.zeros((KROWS, TB), F32)
+
+    def entry(row, at, most):
+        return jnp.minimum(jnp.maximum(order_ref[row, at], 0), most)
 
     def edge(g):
         rsum, csum = erow[g * 4], ecol[g * 4]
         for i in range(4):
             m = g * 4 + i
-            k = order_ref[0, m]
+            k = entry(0, m, tiles - 1)
             yk = counts_ref[k].astype(F32).astype(BF16)
             rsum += jnp.dot(yk, nt_ref[blocks_ref[1, k]], preferred_element_type=F32)
             erow[m + 1] = rsum
-            k = order_ref[1, m]
+            k = entry(1, m, tiles - 1)
             yk = counts_ref[k].astype(F32).astype(BF16)
             csum += jnp.dot(st_ref[blocks_ref[0, k]], yk, preferred_element_type=F32)
             ecol[m + 1] = csum
@@ -306,7 +296,7 @@
     def place_cols(g):
         for i in range(4):
             t = g * 4 + i
-            cacc[:, pl.ds(pl.multiple_of(t * TB, TB), TB)] += ecol[start_ref[1, t + 1]] - ecol[start_ref[1, t]]
+            cacc[:, pl.ds(pl.multiple_of(t * TB, TB), TB)] += ecol[entry(3, t + 1, tiles)] - ecol[entry(3, t, tiles)]
 
     spans(cacc.shape[1] // TB // 4, place_cols)
 
@@ -318,7 +308,7 @@
         for h in range(2):
             t = (z + NZ - ORDER[slot]) % NZ * 2 + h
             acc = racc[pl.ds(slot * 256 + h * TB, TB), :]
-            parts.append(acc + erow[start_ref[0, t + 1]] - erow[start_ref[0, t]])
+            parts.append(acc + erow[entry(2, t + 1, tiles)] - erow[entry(2, t, tiles)])
         return centred(jnp.concatenate(parts, axis=0).T[0:KROWS], s_ref[:, pl.ds(slot * 256, 256)])
 
     rget = {}
@@ -342,7 +332,7 @@
     def rows_late(i):
         e = NZ - LATE[i]
         for t, p in enumerate(pack(rows_done(SLOT[LATE[i]]))):
-            lout[i, t] = p
+            lout[i, t, 0:PIECE] = p.astype(BF16)
         for d in range(NY):
             peer = {"row": lax.axis_index("row"), "col": (z + e) % NZ * NY + (y + d) % NY}
             late[i, d] = send(lout.at[i, (y + d) % NY], lin.at[i, d], l_send.at[i, d], l_recv.at[i, d], peer)
@@ -376,23 +366,21 @@
     cols_units(2, 1, 2, 1 - core)
     cols_other(2)
     cols_units(2, 1, 2, core)
+    spans(3, lambda i: single(6, chip(3 + i)))
+    rows_out(6)
     cols_sum(2)
     relayed = send(xbuf.at[2], xin.at[2], cx_send.at[2], cx_recv.at[2], onward)
-    spans(3, lambda i: single(6, chip(3 + i)))
-    rows_out(6)
     spans(6, lambda i: pair(1, chip(3 + i // 2) * 2 + i % 2))
     rows_out(2)
     rows_out(3)
     for d in XNEAR:
         cols_units(d, 2, 1, 1 - core)
         cols_other(d)
+    for d in XNEAR:
         cols_units(d, 2, 1, core)
         cols_out(d)
-    cols_units(0, 2, 1, 1 - core)
-    cols_other(0)
-    cols_units(0, 2, 1, core)
+    single(4, x)
     rows_late(0)
-    rows_late(1)
 
     total = rows_done(7)
     for e in (6, 2, 4, 5, 3):
@@ -401,10 +389,13 @@
     for t, p in enumerate(pack(total)):
         yblk[t] = p
     yback = {d: send(yblk.at[(y + d) % NY], yin.at[d], ry_send.at[d], ry_recv.at[d], ys[d]) for d in YD}
-
-    cget[0].wait_recv()
+    single(5, x)
+    cols_other(0)
+    rows_late(1)
+
     for d in XNEAR:
         xget[d].wait_recv()
+    cget[0].wait_recv()
     for h in range(width // 256):
         sl = pl.ds(h * 256, 256)
         acc = columns(cacc, x * 2 + core, width)[0:OROWS, sl] + sib[0, :, sl]
@@ -414,7 +405,7 @@
     own_sums = yblk[y]
     for key in late:
         late[key].wait_recv()
-        own_sums += lin[key]
+        own_sums += lin[key][0:PIECE].astype(F32)
     for d in YD:
         yback[d].wait_recv()
         own_sums += yin[d]
@@ -454,14 +445,14 @@
         scratch_shapes=[
             pltpu.SMEM((2, tiles), jnp.int32), pltpu.SMEM((1, 1), F32), pltpu.VMEM((1, own_rows), BF16),
             pltpu.VMEM((own_cols // 128, 128), BF16), pltpu.VMEM(slab_pos.shape, BF16), pltpu.VMEM(node_pos.shape, BF16),
-            pltpu.VMEM(edge_counts.shape, jnp.int32), dma((7,)),
-            pltpu.SMEM((4, tiles), jnp.int32), pltpu.SMEM((2, cols // TB + 1), jnp.int32),
+            pltpu.VMEM(edge_counts.shape, jnp.int32), dma((9,)),
+            pltpu.VMEM((2, tiles), jnp.int32), pltpu.VMEM((8, 128), jnp.int32), pltpu.SMEM((8, 128), jnp.int32),
             pltpu.VMEM((KROWS, rows), BF16), pltpu.VMEM((KROWS, cols), BF16), pltpu.VMEM((cols // TB, TB, 128), BF16),
             pltpu.VMEM((rows // TB, KROWS, TB), BF16),
             pltpu.VMEM((rows, 256), BF16), pltpu.VMEM((rows, 128), F32), pltpu.VMEM((KROWS, cols), F32),
             pltpu.VMEM((tiles + 1, TB, 128), F32), pltpu.VMEM((tiles + 1, KROWS, TB), F32),
             pltpu.VMEM((NY, KROWS, 128), BF16), *pieces, group, group,
-            pltpu.VMEM((2, NY, PIECE, 128), F32), pltpu.VMEM((2, NY, PIECE, 128), F32),
+            pltpu.VMEM((2, NY, 48, 128), BF16), pltpu.VMEM((2, NY, 48, 128), BF16),
             pltpu.VMEM((NY, PIECE, 128), F32), pltpu.VMEM((NY, PIECE, 128), F32),
         ] + [dma((NX,))] * 4 + [dma((NY,))] * 2 + [dma((NZ,))] * 2
         + [dma((NX,))] * 4 + [dma((NZ,))] * 2 + [dma((2, NY))] * 2 + [dma((NY,))] * 2,

time: 60.8 us -> 59.2 us (0.974)
  Pallas kernels: 59.4 us -> 57.4 us
    pallas_call x1, Pallas kernels: 57.6 us -> 55.6 us  [local(): pl.pallas_call(body, out_shape=(jax.ShapeDtypeStruct((PIECE, 128), F32),...]
where the time goes in v5:
time: 59.2 us; the launch traced here: 58.7 us
  Pallas kernels  57.4 us (97%)
  between operations  1.29 us (2%)
    pallas_call x1, Pallas kernels, local(): pl.pallas_call(body, out_shape=(jax.ShapeDtypeStruct((PIECE, 128), F32),...  55.6 us
    pallas_call x1, Pallas kernels, local(): pl.pallas_call(functools.partial(finish, n_nodes=n_nodes, n_slab=n_slab),...  1.83 us

profile of v5, /device:TPU:1, one launch (start us, length us, event | category | flops | bytes accessed | tf_op | source)
XLA Modules:
  0.0 58.7 jit_solution(3763910820675671033)
XLA Ops:
  1.3 55.6 %gradient.1 = (f32[40,128]{1,0:T(8,128)}, f32[72,1024]{1,0:T(8,128)}) custom-call(s32[2,16]{1,0:T(2,128)} %bitcast.8, f32[1,1]{1,0:T(1,128)} %bitcast.6.alpha_hbm, bf16[1,64]{1,0:T(2,128)(2,1)} %bitcast.9, bf16[8,128]{1,0:T(8,128)(2,1)} %bitcast.7, bf16[64,64]{1,0:T(8,128)(2,1)} %spos_hbm.1, bf16[64,1024]{1,0:T(8,128)(2,1)} %npos_ref.1, ...), custom_call_target="tpu_custom_call" | custom-call | tf_op jit(solution)/shard_map/gradient/pallas_call | solution.py:440
  56.9 1.8 %finish.1 = (f32[64,64]{1,0:T(8,128)}, f32[1,64]{1,0:T(1,128)}, f32[64,1024]{1,0:T(8,128)}, f32[1,1024]{1,0:T(1,128)}) custom-call(bf16[64,1024]{1,0:T(8,128)(2,1)} %npos_ref.1, f32[40,128]{1,0:T(8,128)} %get-tuple-element.10.rows_ref, f32[72,1024]{1,0:T(8,128)} %get-tuple-element.11.cols_ref), custom_call_target="tpu_custom_call" | custom-call | tf_op jit(solution)/shard_map/finish/pallas_call | solution.py:465

commit v6 on v5

--- a/solution.py
+++ b/solution.py
@@ -15,9 +15,9 @@
 XD = YD = (1, 3, 2)
 XNEAR = (1, 3)
 ZD = (1, 7, 2, 6, 3, 5, 4)
-ORDER = (2, 6, 3, 5, 1, 7, 4, 0)
+ORDER = (2, 6, 5, 3, 1, 7, 4, 0)
 ZSEND = (2, 6, 3, 5, 4, 1, 7)
-LATE = (1, 7)
+LATE = (5, 3, 1, 7)
 PIECE = 40
 SLOT = {d: s for s, d in enumerate(ORDER)}
 
@@ -221,8 +221,8 @@
         racc[sl, :] -= jnp.dot(lam, nt, preferred_element_type=F32)
         cacc[:, q] -= jnp.dot(s_ref[:, sl], lam, preferred_element_type=F32)
 
-    def pair(p, j):
-        sweep(p * 512, 512, j * width, width)
+    def pair(c):
+        sweep(0, 512, c * (2 * width), 2 * width)
 
     def single(slot, c):
         sweep(slot * 256, 256, c * (2 * width), 2 * width)
@@ -254,16 +254,16 @@
     for d in ORDER[0:2]:
         zget[d].wait_recv()
         prep_rows(SLOT[d])
-    spans(2, lambda i: pair(0, x * 2 + i))
+    pair(x)
     npass(2)
-    spans(4, lambda i: pair(0, chip(3 + i // 2 * 2) * 2 + i % 2))
+    spans(2, lambda i: pair(chip(3 + i * 2)))
     nready(2)
     for d in XD:
         copies.append(remote(npiece(d, core), npiece(d, core), f_send.at[d], f_recv.at[d], sibling))
     prep_cols(chip(2) * 2)
     prep_cols(chip(2) * 2 + 1)
     single(SLOT[0], chip(2))
-    spans(2, lambda i: pair(0, chip(2) * 2 + i))
+    pair(chip(2))
     for d in ORDER[2:-1]:
         zget[d].wait_recv()
         prep_rows(SLOT[d])
@@ -303,19 +303,19 @@
     def centred(sums, pos):
         return jnp.concatenate([sums[0:64] - pos[0:64].astype(F32) * sums[64:65], sums[64:80]], axis=0)
 
-    def rows_done(slot):
+    def rows_done(slot, d):
         parts = []
         for h in range(2):
-            t = (z + NZ - ORDER[slot]) % NZ * 2 + h
-            acc = racc[pl.ds(slot * 256 + h * TB, TB), :]
+            t = (z + NZ - d) % NZ * 2 + h
+            acc = racc[pl.ds(pl.multiple_of(slot * 256 + h * TB, TB), TB), :]
             parts.append(acc + erow[entry(2, t + 1, tiles)] - erow[entry(2, t, tiles)])
-        return centred(jnp.concatenate(parts, axis=0).T[0:KROWS], s_ref[:, pl.ds(slot * 256, 256)])
+        return centred(jnp.concatenate(parts, axis=0).T[0:KROWS], columns(s_ref, slot, 256)[...])
 
     rget = {}
 
     def rows_out(slot):
         e = (NZ - ORDER[slot]) % NZ
-        zout[e] = rows_done(slot).astype(BF16)
+        zout[e] = rows_done(slot, ORDER[slot]).astype(BF16)
         rget[e] = send(zout.at[e], zin.at[e], rz_send.at[e], rz_recv.at[e], zs[e])
 
     def pack(block):
@@ -327,75 +327,94 @@
             out.append(jnp.where(lane < 64, pltpu.roll(top, 64, 1), low))
         return out
 
-    late = {}
+    def late_copy(i, t):
+        e = NZ - (13 - 2 * i) % NZ
+        peer = {"row": lax.axis_index("row"), "col": (z + e) % NZ * NY + (y + t) % NY}
+        return remote(lout.at[i, (y + t) % NY], lin.at[i, t], l_send.at[i, t], l_recv.at[i, t], peer)
 
     def rows_late(i):
-        e = NZ - LATE[i]
-        for t, p in enumerate(pack(rows_done(SLOT[LATE[i]]))):
+        for t, p in enumerate(pack(rows_done(2 + i, (13 - 2 * i) % NZ))):
             lout[i, t, 0:PIECE] = p.astype(BF16)
-        for d in range(NY):
-            peer = {"row": lax.axis_index("row"), "col": (z + e) % NZ * NY + (y + d) % NY}
-            late[i, d] = send(lout.at[i, (y + d) % NY], lin.at[i, d], l_send.at[i, d], l_recv.at[i, d], peer)
-
-    cget, xget = {}, {}
-
-    def cols_other(d):
+        for t in range(NY):
+            late_copy(i, t).start()
+
+    def core_copy(d):
         src = columns(cacc, chip(d) * 2 + 1 - core, width).at[0:OROWS]
-        cget[d] = send(src, sib.at[d], cf_send.at[d], cf_recv.at[d], sibling)
+        return remote(src, sib.at[d], cf_send.at[d], cf_recv.at[d], sibling)
 
     def cols_sum(d):
-        cget[d].wait_recv()
+        core_copy(d).wait_recv()
         xbuf[d] = columns(cacc, chip(d) * 2 + core, width)[0:OROWS] + sib[d]
 
-    def cols_out(d):
-        cols_sum(d)
-
-        @pl.when(near == d)
-        def _():
-            relayed.wait_recv()
-            xbuf[d] += xin[2]
-
-        xget[d] = send(xbuf.at[d], xin.at[d], cx_send.at[d], cx_recv.at[d], xs[d])
-
-    def cols_units(d, first, n, k):
-        spans(n, lambda i: pair(first + i, chip(d) * 2 + k))
+    def chip_copy(d):
+        peer = {"row": chip(d) * 2 + core, "col": lax.axis_index("col")}
+        return remote(xbuf.at[d], xin.at[d], cx_send.at[d], cx_recv.at[d], peer)
+
+    def four(d, k):
+        sweep(512, 1024, (chip(d) * 2 + k) * width, width)
 
     rows_out(0)
     rows_out(1)
     single(6, chip(2))
-    cols_units(2, 1, 2, 1 - core)
-    cols_other(2)
-    cols_units(2, 1, 2, core)
+    def far_units(i):
+        four(2, (1 + core + i) % 2)
+
+        @pl.when(i == 0)
+        def _():
+            core_copy(2).start()
+
+    spans(2, far_units)
     spans(3, lambda i: single(6, chip(3 + i)))
     rows_out(6)
     cols_sum(2)
     relayed = send(xbuf.at[2], xin.at[2], cx_send.at[2], cx_recv.at[2], onward)
-    spans(6, lambda i: pair(1, chip(3 + i // 2) * 2 + i % 2))
-    rows_out(2)
-    rows_out(3)
-    for d in XNEAR:
-        cols_units(d, 2, 1, 1 - core)
-        cols_other(d)
-    for d in XNEAR:
-        cols_units(d, 2, 1, core)
-        cols_out(d)
-    single(4, x)
-    rows_late(0)
-
-    total = rows_done(7)
-    for e in (6, 2, 4, 5, 3):
+
+    def near_units(i):
+        d = 1 + i % 2 * 2
+        four(d, (1 + core + i // 2) % 2)
+
+        @pl.when(i < 2)
+        def _():
+            core_copy(d).start()
+
+        @pl.when(i >= 2)
+        def _():
+            cols_sum(d)
+
+            @pl.when(near == d)
+            def _():
+                relayed.wait_recv()
+                xbuf[d] += xin[2]
+
+            chip_copy(d).start()
+
+    spans(4, near_units)
+
+    total = rows_done(7, 0)
+    for e in (6, 2, 4):
         rget[e].wait_recv()
         total += zin[e].astype(F32)
     for t, p in enumerate(pack(total)):
         yblk[t] = p
     yback = {d: send(yblk.at[(y + d) % NY], yin.at[d], ry_send.at[d], ry_recv.at[d], ys[d]) for d in YD}
-    single(5, x)
-    cols_other(0)
-    rows_late(1)
+
+    def late_units(i):
+        single(2 + i, x)
+
+        @pl.when(i == 3)
+        def _():
+            core_copy(0).start()
+
+        rows_late(i)
+
+    spans(4, late_units)
 
     for d in XNEAR:
-        xget[d].wait_recv()
-    cget[0].wait_recv()
+        chip_copy(d).wait_recv()
+        copies.append(chip_copy(d))
+    core_copy(0).wait_recv()
+    for d in range(NX):
+        copies.append(core_copy(d))
     for h in range(width // 256):
         sl = pl.ds(h * 256, 256)
         acc = columns(cacc, x * 2 + core, width)[0:OROWS, sl] + sib[0, :, sl]
@@ -403,9 +422,11 @@
         cout_ref[:, sl] = acc
 
     own_sums = yblk[y]
-    for key in late:
-        late[key].wait_recv()
-        own_sums += lin[key][0:PIECE].astype(F32)
+    for i in range(len(LATE)):
+        for t in range(NY):
+            late_copy(i, t).wait_recv()
+            copies.append(late_copy(i, t))
+            own_sums += lin[i, t, 0:PIECE].astype(F32)
     for d in YD:
         yback[d].wait_recv()
         own_sums += yin[d]
@@ -452,10 +473,10 @@
             pltpu.VMEM((rows, 256), BF16), pltpu.VMEM((rows, 128), F32), pltpu.VMEM((KROWS, cols), F32),
             pltpu.VMEM((tiles + 1, TB, 128), F32), pltpu.VMEM((tiles + 1, KROWS, TB), F32),
             pltpu.VMEM((NY, KROWS, 128), BF16), *pieces, group, group,
-            pltpu.VMEM((2, NY, 48, 128), BF16), pltpu.VMEM((2, NY, 48, 128), BF16),
+            pltpu.VMEM((len(LATE), NY, 48, 128), BF16), pltpu.VMEM((len(LATE), NY, 48, 128), BF16),
             pltpu.VMEM((NY, PIECE, 128), F32), pltpu.VMEM((NY, PIECE, 128), F32),
         ] + [dma((NX,))] * 4 + [dma((NY,))] * 2 + [dma((NZ,))] * 2
-        + [dma((NX,))] * 4 + [dma((NZ,))] * 2 + [dma((2, NY))] * 2 + [dma((NY,))] * 2,
+        + [dma((NX,))] * 4 + [dma((NZ,))] * 2 + [dma((len(LATE), NY))] * 2 + [dma((NY,))] * 2,
         compiler_params=params(collective_id=0, has_side_effects=True),
         name="gradient",
     )(

time: 59.2 us -> 58.6 us (0.990)
  the two profiles are of different devices: /device:TPU:1 before, /device:TPU:32 now
where the time goes in v6:
time: 58.6 us; the launch traced here: 58.4 us
  Pallas kernels  57.1 us (97%)
  between operations  1.29 us (2%)
    pallas_call x1, Pallas kernels, local(): pl.pallas_call(body, out_shape=(jax.ShapeDtypeStruct((PIECE, 128), F32),...  55.3 us
    pallas_call x1, Pallas kernels, local(): pl.pallas_call(functools.partial(finish, n_nodes=n_nodes, n_slab=n_slab),...  1.83 us

profile of v6, /device:TPU:32, one launch (start us, length us, event | category | flops | bytes accessed | tf_op | source)
XLA Modules:
  0.0 58.4 jit_solution(5833628809275075627)
XLA Ops:
  1.3 55.3 %gradient.1 = (f32[40,128]{1,0:T(8,128)}, f32[72,1024]{1,0:T(8,128)}) custom-call(s32[2,16]{1,0:T(2,128)} %bitcast.8, f32[1,1]{1,0:T(1,128)} %bitcast.6.alpha_hbm, bf16[1,64]{1,0:T(2,128)(2,1)} %bitcast.9, bf16[8,128]{1,0:T(8,128)(2,1)} %bitcast.7, bf16[64,64]{1,0:T(8,128)(2,1)} %spos_hbm.1, bf16[64,1024]{1,0:T(8,128)(2,1)} %npos_ref.1, ...), custom_call_target="tpu_custom_call" | custom-call | tf_op jit(solution)/shard_map/gradient/pallas_call | solution.py:461
  56.6 1.8 %finish.1 = (f32[64,64]{1,0:T(8,128)}, f32[1,64]{1,0:T(1,128)}, f32[64,1024]{1,0:T(8,128)}, f32[1,1024]{1,0:T(1,128)}) custom-call(bf16[64,1024]{1,0:T(8,128)(2,1)} %npos_ref.1, f32[40,128]{1,0:T(8,128)} %get-tuple-element.10.rows_ref, f32[72,1024]{1,0:T(8,128)} %get-tuple-element.11.cols_ref), custom_call_target="tpu_custom_call" | custom-call | tf_op jit(solution)/shard_map/finish/pallas_call | solution.py:486

commit v7 on v6

--- a/solution.py
+++ b/solution.py
@@ -17,7 +17,7 @@
 ZD = (1, 7, 2, 6, 3, 5, 4)
 ORDER = (2, 6, 5, 3, 1, 7, 4, 0)
 ZSEND = (2, 6, 3, 5, 4, 1, 7)
-LATE = (5, 3, 1, 7)
+LATE = (1, 7)
 PIECE = 40
 SLOT = {d: s for s, d in enumerate(ORDER)}
 
@@ -328,12 +328,12 @@
         return out
 
     def late_copy(i, t):
-        e = NZ - (13 - 2 * i) % NZ
+        e = NZ - (9 - 2 * i) % NZ
         peer = {"row": lax.axis_index("row"), "col": (z + e) % NZ * NY + (y + t) % NY}
         return remote(lout.at[i, (y + t) % NY], lin.at[i, t], l_send.at[i, t], l_recv.at[i, t], peer)
 
     def rows_late(i):
-        for t, p in enumerate(pack(rows_done(2 + i, (13 - 2 * i) % NZ))):
+        for t, p in enumerate(pack(rows_done(4 + i, (9 - 2 * i) % NZ))):
             lout[i, t, 0:PIECE] = p.astype(BF16)
         for t in range(NY):
             late_copy(i, t).start()
@@ -371,7 +371,7 @@
 
     def near_units(i):
         d = 1 + i % 2 * 2
-        four(d, (1 + core + i // 2) % 2)
+        sweep(1024, 512, (chip(d) * 2 + (1 + core + i // 2) % 2) * width, width)
 
         @pl.when(i < 2)
         def _():
@@ -388,26 +388,35 @@
 
             chip_copy(d).start()
 
+    spans(3, lambda i: sweep(512, 512, chip(3 + i) * (2 * width), 2 * width))
+    rows_out(2)
+    rows_out(3)
     spans(4, near_units)
 
-    total = rows_done(7, 0)
-    for e in (6, 2, 4):
-        rget[e].wait_recv()
-        total += zin[e].astype(F32)
-    for t, p in enumerate(pack(total)):
-        yblk[t] = p
-    yback = {d: send(yblk.at[(y + d) % NY], yin.at[d], ry_send.at[d], ry_recv.at[d], ys[d]) for d in YD}
+    def y_copy(d):
+        return remote(yblk.at[(y + d) % NY], yin.at[d], ry_send.at[d], ry_recv.at[d], ys[d])
 
     def late_units(i):
-        single(2 + i, x)
-
-        @pl.when(i == 3)
+        single(4 + i, x)
+
+        @pl.when(i == 1)
         def _():
             core_copy(0).start()
 
         rows_late(i)
 
-    spans(4, late_units)
+        @pl.when(i == 0)
+        def _():
+            total = rows_done(7, 0)
+            for e in (6, 2, 4, 5, 3):
+                rget[e].wait_recv()
+                total += zin[e].astype(F32)
+            for t, p in enumerate(pack(total)):
+                yblk[t] = p
+            for d in YD:
+                y_copy(d).start()
+
+    spans(2, late_units)
 
     for d in XNEAR:
         chip_copy(d).wait_recv()
@@ -428,7 +437,8 @@
             copies.append(late_copy(i, t))
             own_sums += lin[i, t, 0:PIECE].astype(F32)
     for d in YD:
-        yback[d].wait_recv()
+        y_copy(d).wait_recv()
+        copies.append(y_copy(d))
         own_sums += yin[d]
     rout_ref[...] = own_sums
     for c in copies:

time: 58.6 us -> 57.6 us (0.983)
  the two profiles are of different devices: /device:TPU:32 before, /device:TPU:1 now
where the time goes in v7:
time: 57.6 us; the launch traced here: 57.4 us
  Pallas kernels  56.1 us (97%)
  between operations  1.29 us (2%)
    pallas_call x1, Pallas kernels, local(): pl.pallas_call(body, out_shape=(jax.ShapeDtypeStruct((PIECE, 128), F32),...  54.3 us
    pallas_call x1, Pallas kernels, local(): pl.pallas_call(functools.partial(finish, n_nodes=n_nodes, n_slab=n_slab),...  1.83 us

profile of v7, /device:TPU:1, one launch (start us, length us, event | category | flops | bytes accessed | tf_op | source)
XLA Modules:
  0.0 57.4 jit_solution(13446942413025612456)
XLA Ops:
  1.3 54.3 %gradient.1 = (f32[40,128]{1,0:T(8,128)}, f32[72,1024]{1,0:T(8,128)}) custom-call(s32[2,16]{1,0:T(2,128)} %bitcast.8, f32[1,1]{1,0:T(1,128)} %bitcast.6.alpha_hbm, bf16[1,64]{1,0:T(2,128)(2,1)} %bitcast.9, bf16[8,128]{1,0:T(8,128)(2,1)} %bitcast.7, bf16[64,64]{1,0:T(8,128)(2,1)} %spos_hbm.1, bf16[64,1024]{1,0:T(8,128)(2,1)} %npos_ref.1, ...), custom_call_target="tpu_custom_call" | custom-call | tf_op jit(solution)/shard_map/gradient/pallas_call | solution.py:471
  55.6 1.8 %finish.1 = (f32[64,64]{1,0:T(8,128)}, f32[1,64]{1,0:T(1,128)}, f32[64,1024]{1,0:T(8,128)}, f32[1,1024]{1,0:T(1,128)}) custom-call(bf16[64,1024]{1,0:T(8,128)(2,1)} %npos_ref.1, f32[40,128]{1,0:T(8,128)} %get-tuple-element.10.rows_ref, f32[72,1024]{1,0:T(8,128)} %get-tuple-element.11.cols_ref), custom_call_target="tpu_custom_call" | custom-call | tf_op jit(solution)/shard_map/finish/pallas_call | solution.py:496
